TPU v7x, 256 devices: a whole 4x4x8 slice. The times are simulated.
256 devices in a mesh: chan: 8 (over y, core), ctx: 32 (over x, z).
Axes of the slice: x: 4, y: 4, z: 8, core: 2. Of those that a mesh axis runs over, the one named last changes fastest.
Arguments:
- x_one: bfloat16 [4096, 4096], P('ctx', 'chan'), may hold values from -6 to 6
- x_two: bfloat16 [4096, 4096], P('ctx', 'chan'), may hold values from -6 to 6
- values: bfloat16 [4096, 4096], P('ctx', 'chan'), may hold values from -6 to 6
- grad_out: bfloat16 [4096, 4096], P('ctx', 'chan'), may hold values from -6 to 6
- filter_spectrum: float32 [2, 2, 32, 128, 4096], P(None, None, 'ctx', None, 'chan'), may hold values from -6 to 6
- skip_gain: float32 [4096], P('chan'), may hold values from -4 to 4
Outputs:
- d_one: bfloat16 [4096, 4096], P('ctx', 'chan')
- d_two: bfloat16 [4096, 4096], P('ctx', 'chan')
- d_values: bfloat16 [4096, 4096], P('ctx', 'chan')
- d_filter: float32 [2, 2, 32, 128, 4096], P(None, None, 'ctx', None, 'chan')
- d_skip: float32 [4096], P('chan')
All inputs are finite; a program needn't handle non-finite values.
Results may differ from a plain program's by a relative error of at most 0.0011.
Values sent between devices are 32-bit elements; how exact they have to be, the bound alone decides.
No kernel may reach another device: no remote copies, remote signals or barrier semaphores. Data moves between devices by JAX's collectives and lax.ppermute only.
A program may use at most 64 MiB of HBM per device.

v0:
```python
import math

import jax
import jax.numpy as jnp
import numpy as np
from jax import lax
from jax.sharding import PartitionSpec as P

PRECISE = lax.Precision.HIGHEST
TWO_PI = 2.0 * math.pi


def swapped_2(value, axis, apart):
    mask = 2**apart
    pairs = [(source, source ^ mask) for source in range(lax.axis_size(axis))]
    return lax.ppermute(value, axis, pairs)


def reversed_order(total_count):
    digits = total_count.bit_length() - 1
    order_list = []
    for position in range(total_count):
        flipped = 0
        for bit_place in range(digits):
            flipped = flipped | (position >> bit_place & 1) << digits - 1 - bit_place
        order_list.append(flipped)
    return np.array(order_list, dtype=np.int32)


def phase_grid(left_index, right_index, modulus):
    product = left_index[:, None] * right_index[None, :] % modulus
    return TWO_PI * product.astype(jnp.float32) / modulus


def butterfly_forward(stacked, groups, device):
    digits = groups.bit_length() - 1
    real_part = stacked
    imag_part = jnp.zeros_like(stacked)
    for bit_level in range(digits - 1, -1, -1):
        half_span = 1 << bit_level
        span_size = 2 * half_span
        offset = device % span_size
        is_upper = offset >= half_span
        angles = -TWO_PI * (offset - half_span).astype(jnp.float32) / span_size
        if bit_level == digits - 1:
            other_re = swapped_2(real_part, "ctx", bit_level)
            other_im = jnp.zeros_like(other_re)
        else:
            swapped = swapped_2(jnp.stack([real_part, imag_part]), "ctx", bit_level)
            other_re = swapped[0]
            other_im = swapped[1]
        diff_re = other_re - real_part
        diff_im = other_im - imag_part
        cosine = jnp.cos(angles)
        sine_val = jnp.sin(angles)
        upper_re = diff_re * cosine - diff_im * sine_val
        upper_im = diff_re * sine_val + diff_im * cosine
        real_part = jnp.where(is_upper, upper_re, real_part + other_re)
        imag_part = jnp.where(is_upper, upper_im, imag_part + other_im)
    return (real_part, imag_part)


def butterfly_inverse(real_part, imag_part, groups, device):
    digits = groups.bit_length() - 1
    for bit_level in range(digits):
        half_span = 1 << bit_level
        span_size = 2 * half_span
        offset = device % span_size
        is_upper = offset >= half_span
        turn_step = offset % half_span
        angles = TWO_PI * turn_step.astype(jnp.float32) / span_size
        cosine = jnp.cos(angles)
        sine_val = jnp.sin(angles)
        swapped = swapped_2(jnp.stack([real_part, imag_part]), "ctx", bit_level)
        other_re = swapped[0]
        other_im = swapped[1]
        lower_re = real_part + cosine * other_re - sine_val * other_im
        lower_im = imag_part + cosine * other_im + sine_val * other_re
        upper_re = other_re - (cosine * real_part - sine_val * imag_part)
        upper_im = other_im - (cosine * imag_part + sine_val * real_part)
        real_part = jnp.where(is_upper, upper_re, lower_re)
        imag_part = jnp.where(is_upper, upper_im, lower_im)
    return (real_part, imag_part)


def per_device(x_one, x_two, values, grad_out, filter_spectrum, skip_gain):
    groups = lax.axis_size("ctx")
    device = lax.axis_index("ctx")
    rows_local = x_one.shape[0]
    seq_total = groups * rows_local
    double_len = 2 * seq_total
    order_list = jnp.asarray(reversed_order(groups))
    owner_freq = order_list[device]
    grad_prod = grad_out.astype(jnp.float32) * x_two.astype(jnp.float32)
    signal = x_one.astype(jnp.float32) * values.astype(jnp.float32)
    d_skip = lax.psum(jnp.sum(grad_prod * signal, axis=0), "ctx")
    local_rows = jnp.arange(rows_local, dtype=jnp.int32)
    positions = device * rows_local + local_rows
    pad_angle = TWO_PI * positions.astype(jnp.float32) / double_len
    pad_cos = jnp.cos(pad_angle)[:, None]
    pad_sin = jnp.sin(pad_angle)[:, None]
    stacked = jnp.stack(
        [
            grad_prod,
            signal,
            grad_prod * pad_cos,
            signal * pad_cos,
            grad_prod * pad_sin,
            signal * pad_sin,
        ]
    )
    spec_re, spec_im = butterfly_forward(stacked, groups, device)
    twist = phase_grid(owner_freq[None], local_rows, seq_total)[0][None, :, None]
    spec_re, spec_im = (
        spec_re * jnp.cos(twist) + spec_im * jnp.sin(twist),
        spec_im * jnp.cos(twist) - spec_re * jnp.sin(twist),
    )
    big_phase = phase_grid(local_rows, local_rows, rows_local)
    big_cos = jnp.cos(big_phase)
    big_sin = jnp.sin(big_phase)
    freq_re = jnp.einsum("bm,kmc->kbc", big_cos, spec_re, precision=PRECISE) + jnp.einsum(
        "bm,kmc->kbc", big_sin, spec_im, precision=PRECISE
    )
    freq_im = jnp.einsum("bm,kmc->kbc", big_cos, spec_im, precision=PRECISE) - jnp.einsum(
        "bm,kmc->kbc", big_sin, spec_re, precision=PRECISE
    )
    grad_re = jnp.stack([freq_re[0], freq_re[2] + freq_im[4]])
    grad_im = jnp.stack([freq_im[0], freq_im[2] - freq_re[4]])
    sig_re = jnp.stack([freq_re[1], freq_re[3] + freq_im[5]])
    sig_im = jnp.stack([freq_im[1], freq_im[3] - freq_re[5]])
    filt_re = filter_spectrum[0, :, 0]
    filt_im = filter_spectrum[1, :, 0]
    d_filter = (
        jnp.stack([sig_re * grad_re + sig_im * grad_im, sig_re * grad_im - sig_im * grad_re])[
            :, :, None
        ]
        / double_len
    )
    conv_re = filt_re * sig_re - filt_im * sig_im
    conv_im = filt_re * sig_im + filt_im * sig_re
    back_re = filt_re * grad_re + filt_im * grad_im
    back_im = filt_re * grad_im - filt_im * grad_re
    inv_re = jnp.concatenate([conv_re, back_re], axis=0)
    inv_im = jnp.concatenate([conv_im, back_im], axis=0)
    time_re = jnp.einsum("mb,kbc->kmc", big_cos, inv_re, precision=PRECISE) - jnp.einsum(
        "mb,kbc->kmc", big_sin, inv_im, precision=PRECISE
    )
    time_im = jnp.einsum("mb,kbc->kmc", big_cos, inv_im, precision=PRECISE) + jnp.einsum(
        "mb,kbc->kmc", big_sin, inv_re, precision=PRECISE
    )
    twist_back = phase_grid(owner_freq[None], local_rows, seq_total)[0][None, :, None]
    rot_re = time_re * jnp.cos(twist_back) - time_im * jnp.sin(twist_back)
    rot_im = time_im * jnp.cos(twist_back) + time_re * jnp.sin(twist_back)
    out_re, out_im = butterfly_inverse(rot_re, rot_im, groups, device)
    conv = (out_re[0] + pad_cos * out_re[1] - pad_sin * out_im[1]) / double_len
    back = (out_re[2] + pad_cos * out_re[3] - pad_sin * out_im[3]) / double_len
    d_signal = back + skip_gain[None, :] * grad_prod
    d_one = (d_signal * values.astype(jnp.float32)).astype(jnp.bfloat16)
    d_values = (d_signal * x_one.astype(jnp.float32)).astype(jnp.bfloat16)
    d_two = (grad_out.astype(jnp.float32) * (conv + skip_gain[None, :] * signal)).astype(
        jnp.bfloat16
    )
    return (d_one, d_two, d_values, d_filter, d_skip)


def solution(mesh):
    return jax.shard_map(
        per_device,
        mesh=mesh,
        in_specs=(
            P("ctx", "chan"),
            P("ctx", "chan"),
            P("ctx", "chan"),
            P("ctx", "chan"),
            P(None, None, "ctx", None, "chan"),
            P("chan"),
        ),
        out_specs=(
            P("ctx", "chan"),
            P("ctx", "chan"),
            P("ctx", "chan"),
            P(None, None, "ctx", None, "chan"),
            P("chan"),
        ),
        check_vma=False,
    )
```

profile of v0, /device:TPU:16, one launch (start us, length us, event | category | flops | bytes accessed | tf_op | source)
XLA Modules:
  0.0 914.0 jit_solution(16419959004524142355)
XLA Ops:
  1.7 1.0 copy.14
  2.7 1.0 copy.16
  3.7 1.0 copy.15
  5.5 3.1 collective-permute-start
  8.7 34.5 %collective-permute-done = f32[6,128,512]{1,2,0:T(8,128)S(1)} collective-permute-done((f32[6,128,512]{1,2,0:T(8,128)S(1)}, f32[6,128,512]{1,2,0:T(8,128)S(1)}, u32[]{:S(2)}, u32[]{:S(2)}) %collective-permute-start) | collective-permute-done | bytes 1572896 | tf_op jit(solution)/shard_map/ppermute | solution.py:16
  44.6 1.6 collective-permute-start.1
  46.3 67.4 %collective-permute-done.1 = f32[2,6,128,512]{2,3,1,0:T(8,128)} collective-permute-done((f32[2,6,128,512]{2,3,1,0:T(8,128)S(1)}, f32[2,6,128,512]{2,3,1,0:T(8,128)}, u32[]{:S(2)}, u32[]{:S(2)}) %collective-permute-start.1) | collective-permute-done | bytes 3145760 | tf_op jit(solution)/shard_map/ppermute | solution.py:16
  113.7 3.9 add_select_fusion.6
  117.6 1.9 pad_maximum_fusion.1
  119.5 7.2 collective-permute-start.2
  126.8 133.4 %collective-permute-done.2 = f32[2,6,128,512]{2,3,1,0:T(8,128)} collective-permute-done((f32[2,6,128,512]{2,3,1,0:T(8,128)}, f32[2,6,128,512]{2,3,1,0:T(8,128)}, u32[]{:S(2)}, u32[]{:S(2)}) %collective-permute-start.2) | collective-permute-done | bytes 3145760 | tf_op jit(solution)/shard_map/ppermute | solution.py:16
  260.2 2.5 add_select_fusion.4
  264.5 2.6 collective-permute-start.3
  267.3 132.5 %collective-permute-done.3 = f32[2,6,128,512]{2,3,1,0:T(8,128)} collective-permute-done((f32[2,6,128,512]{2,3,1,0:T(8,128)S(1)}, f32[2,6,128,512]{2,3,1,0:T(8,128)}, u32[]{:S(2)}, u32[]{:S(2)}) %collective-permute-start.3) | collective-permute-done | bytes 3145760 | tf_op jit(solution)/shard_map/ppermute | solution.py:16
  399.8 3.5 add_select_fusion.2
  403.3 1.9 pad_maximum_fusion.3
  405.3 2.2 fusion.108
  407.6 2.1 copy.22
  409.6 2.0 copy.23
  412.9 62.6 %collective-permute-done.4 = f32[2,6,128,512]{2,3,1,0:T(8,128)} collective-permute-done((f32[2,6,128,512]{2,3,1,0:T(8,128)}, f32[2,6,128,512]{2,3,1,0:T(8,128)}, u32[]{:S(2)}, u32[]{:S(2)}) %collective-permute-start.4) | collective-permute-done | bytes 3145760 | tf_op jit(solution)/shard_map/ppermute | solution.py:16
  475.5 2.5 add_select_fusion
  478.0 1.7 fusion.23
  479.8 1.7 fusion.24
  481.5 1.7 subtract_bitcast_fusion
  483.2 1.7 add_bitcast_fusion
  485.0 1.1 slice_bitcast_fusion.27
  487.1 1.2 fusion.16
  488.3 1.2 fusion.17
  489.5 1.5 convolution_subtract_fusion
  491.0 1.4 multiply_subtract_fusion.1
  493.0 46.4 %collective-permute-done.5 = f32[2,4,128,512]{2,3,1,0:T(8,128)S(1)} collective-permute-done((f32[2,4,128,512]{2,3,1,0:T(8,128)S(1)}, f32[2,4,128,512]{2,3,1,0:T(8,128)S(1)}, u32[]{:S(2)}, u32[]{:S(2)}) %collective-permute-start.5) | collective-permute-done | bytes 2097184 | tf_op jit(solution)/shard_map/ppermute | solution.py:16
  539.8 1.5 pad_maximum_fusion.5
  541.5 91.8 %collective-permute-done.6 = f32[2,4,128,512]{2,3,1,0:T(8,128)} collective-permute-done((f32[2,4,128,512]{2,3,1,0:T(8,128)}, f32[2,4,128,512]{2,3,1,0:T(8,128)}, u32[]{:S(2)}, u32[]{:S(2)}) %collective-permute-start.6) | collective-permute-done | bytes 2097184 | tf_op jit(solution)/shard_map/ppermute | solution.py:16
  633.4 2.2 subtract_select_fusion.3
  635.5 1.6 pad_maximum_fusion.6
  637.2 2.6 collective-permute-start.7
  639.9 92.8 %collective-permute-done.7 = f32[2,4,128,512]{2,3,1,0:T(8,128)S(1)} collective-permute-done((f32[2,4,128,512]{2,3,1,0:T(8,128)}, f32[2,4,128,512]{2,3,1,0:T(8,128)S(1)}, u32[]{:S(2)}, u32[]{:S(2)}) %collective-permute-start.7) | collective-permute-done | bytes 2097184 | tf_op jit(solution)/shard_map/ppermute | solution.py:16
  732.7 1.8 subtract_select_fusion.2
  735.9 1.5 collective-permute-start.8
  737.6 46.0 %collective-permute-done.8 = f32[2,4,128,512]{2,3,1,0:T(8,128)} collective-permute-done((f32[2,4,128,512]{2,3,1,0:T(8,128)S(1)}, f32[2,4,128,512]{2,3,1,0:T(8,128)}, u32[]{:S(2)}, u32[]{:S(2)}) %collective-permute-start.8) | collective-permute-done | bytes 2097184 | tf_op jit(solution)/shard_map/ppermute | solution.py:16
  783.6 2.8 subtract_select_fusion.1
  786.4 1.5 pad_maximum_fusion.8
  787.9 3.0 collective-permute-start.9
  791.0 1.3 add_bitcast_fusion.1
  792.4 1.3 copy.21
  793.7 42.7 %collective-permute-done.9 = f32[2,4,128,512]{2,3,1,0:T(8,128)} collective-permute-done((f32[2,4,128,512]{2,3,1,0:T(8,128)}, f32[2,4,128,512]{2,3,1,0:T(8,128)}, u32[]{:S(2)}, u32[]{:S(2)}) %collective-permute-start.9) | collective-permute-done | bytes 2097184 | tf_op jit(solution)/shard_map/ppermute | solution.py:16
  836.4 2.2 subtract_select_fusion
  841.3 72.7 %psum.7 = f32[512]{0:T(512)} all-reduce(f32[512]{0:T(512)S(1)} %get-tuple-element.61), channel_id=1, replica_groups=mesh['chan'=8,'ctx'=32] {'ctx'}, use_global_device_ids=true, to_apply=%region_1.0 | all-reduce | flops 512 | bytes 4096 | tf_op jit(solution)/shard_map/psum | solution.py:96
  (68 shorter events, 12.1 us)
Async XLA Ops:
  4.8 0.7 copy-start.7
  5.5 38.2 %copy-start.5 = (f32[6,128,512]{1,2,0:T(8,128)}, f32[6,128,512]{1,2,0:T(8,128)S(1)}, u32[]{:S(2)}) copy-start(f32[6,128,512]{1,2,0:T(8,128)S(1)} %bitcast_dynamic-update-slice_fusion) | copy-start | bytes 4718596
  5.5 37.7 %collective-permute-start = (f32[6,128,512]{1,2,0:T(8,128)S(1)}, f32[6,128,512]{1,2,0:T(8,128)S(1)}, u32[]{:S(2)}, u32[]{:S(2)}) collective-permute-start(f32[6,128,512]{1,2,0:T(8,128)S(1)} %bitcast_dynamic-update-slice_fusion), channel_id=1, source_target_pairs={{0,16},{1,17},{2,18},{3,19},{4,20},{5,21},{6,22},{7,23},{8,24},{9,... | collective-permute-start | bytes 4718600 | tf_op jit(solution)/shard_map/ppermute | solution.py:16
  43.2 1.1 copy-start.6
  44.6 69.2 %collective-permute-start.1 = (f32[2,6,128,512]{2,3,1,0:T(8,128)S(1)}, f32[2,6,128,512]{2,3,1,0:T(8,128)}, u32[]{:S(2)}, u32[]{:S(2)}) collective-permute-start(f32[2,6,128,512]{2,3,1,0:T(8,128)S(1)} %pad_maximum_fusion), channel_id=1, source_target_pairs={{0,8},{1,9},{2,10},{3,11},{4,12},{5,13},{6,14},{7,15},{8,0},{9,1},... | collective-permute-start | bytes 9437192 | tf_op jit(solution)/shard_map/ppermute | solution.py:16
  119.5 140.8 %collective-permute-start.2 = (f32[2,6,128,512]{2,3,1,0:T(8,128)}, f32[2,6,128,512]{2,3,1,0:T(8,128)}, u32[]{:S(2)}, u32[]{:S(2)}) collective-permute-start(f32[2,6,128,512]{2,3,1,0:T(8,128)} %pad_maximum_fusion.1), channel_id=1, source_target_pairs={{0,4},{1,5},{2,6},{3,7},{4,0},{5,1},{6,2},{7,3},{8,12},{9,13},{10,... | collective-permute-start | bytes 9437192 | tf_op jit(solution)/shard_map/ppermute | solution.py:16
  262.8 1.1 copy-start
  262.8 1.7 copy-start.1
  264.5 135.3 %collective-permute-start.3 = (f32[2,6,128,512]{2,3,1,0:T(8,128)S(1)}, f32[2,6,128,512]{2,3,1,0:T(8,128)}, u32[]{:S(2)}, u32[]{:S(2)}) collective-permute-start(f32[2,6,128,512]{2,3,1,0:T(8,128)S(1)} %pad_maximum_fusion.2), channel_id=1, source_target_pairs={{0,2},{1,3},{2,0},{3,1},{4,6},{5,7},{6,4},{7,5},{8,10},{9,11},{10,... | collective-permute-start | bytes 9437192 | tf_op jit(solution)/shard_map/ppermute | solution.py:16
  405.2 70.3 %collective-permute-start.4 = (f32[2,6,128,512]{2,3,1,0:T(8,128)}, f32[2,6,128,512]{2,3,1,0:T(8,128)}, u32[]{:S(2)}, u32[]{:S(2)}) collective-permute-start(f32[2,6,128,512]{2,3,1,0:T(8,128)} %pad_maximum_fusion.3), channel_id=1, source_target_pairs={{0,1},{1,0},{2,3},{3,2},{4,5},{5,4},{6,7},{7,6},{8,9},{9,8},{10,11... | collective-permute-start | bytes 9437192 | tf_op jit(solution)/shard_map/ppermute | solution.py:16
  407.6 4.1 copy-start.20
  484.9 1.2 copy-start.17
  484.9 1.6 copy-start.18
  486.1 0.7 copy-start.9
  486.1 0.8 copy-start.11
  486.1 0.9 copy-start.13
  486.1 1.0 copy-start.15
  492.6 46.8 %collective-permute-start.5 = (f32[2,4,128,512]{2,3,1,0:T(8,128)S(1)}, f32[2,4,128,512]{2,3,1,0:T(8,128)S(1)}, u32[]{:S(2)}, u32[]{:S(2)}) collective-permute-start(f32[2,4,128,512]{2,3,1,0:T(8,128)S(1)} %pad_maximum_fusion.4), channel_id=1, source_target_pairs={{0,1},{1,0},{2,3},{3,2},{4,5},{5,4},{6,7},{7,6},{8,9},{9,8},{10,11... | collective-permute-start | bytes 6291464 | tf_op jit(solution)/shard_map/ppermute | solution.py:16
  541.4 92.0 %collective-permute-start.6 = (f32[2,4,128,512]{2,3,1,0:T(8,128)}, f32[2,4,128,512]{2,3,1,0:T(8,128)}, u32[]{:S(2)}, u32[]{:S(2)}) collective-permute-start(f32[2,4,128,512]{2,3,1,0:T(8,128)} %pad_maximum_fusion.5), channel_id=1, source_target_pairs={{0,2},{1,3},{2,0},{3,1},{4,6},{5,7},{6,4},{7,5},{8,10},{9,11},{10,... | collective-permute-start | bytes 6291464 | tf_op jit(solution)/shard_map/ppermute | solution.py:16
  635.5 1.7 copy-start.2
  637.2 95.5 %collective-permute-start.7 = (f32[2,4,128,512]{2,3,1,0:T(8,128)}, f32[2,4,128,512]{2,3,1,0:T(8,128)S(1)}, u32[]{:S(2)}, u32[]{:S(2)}) collective-permute-start(f32[2,4,128,512]{2,3,1,0:T(8,128)} %pad_maximum_fusion.6), channel_id=1, source_target_pairs={{0,4},{1,5},{2,6},{3,7},{4,0},{5,1},{6,2},{7,3},{8,12},{9,13},{10,... | collective-permute-start | bytes 6291464 | tf_op jit(solution)/shard_map/ppermute | solution.py:16
  734.5 1.0 copy-start.3
  734.6 1.3 copy-start.4
  735.9 47.7 %collective-permute-start.8 = (f32[2,4,128,512]{2,3,1,0:T(8,128)S(1)}, f32[2,4,128,512]{2,3,1,0:T(8,128)}, u32[]{:S(2)}, u32[]{:S(2)}) collective-permute-start(f32[2,4,128,512]{2,3,1,0:T(8,128)S(1)} %pad_maximum_fusion.7), channel_id=1, source_target_pairs={{0,8},{1,9},{2,10},{3,11},{4,12},{5,13},{6,14},{7,15},{8,0},{9,1},... | collective-permute-start | bytes 6291464 | tf_op jit(solution)/shard_map/ppermute | solution.py:16
  786.3 4.7 copy-start.10
  786.4 4.7 copy-start.12
  786.4 4.7 copy-start.14
  786.4 4.7 copy-start.16
  787.9 48.5 %collective-permute-start.9 = (f32[2,4,128,512]{2,3,1,0:T(8,128)}, f32[2,4,128,512]{2,3,1,0:T(8,128)}, u32[]{:S(2)}, u32[]{:S(2)}) collective-permute-start(f32[2,4,128,512]{2,3,1,0:T(8,128)} %pad_maximum_fusion.8), channel_id=1, source_target_pairs={{0,16},{1,17},{2,18},{3,19},{4,20},{5,21},{6,22},{7,23},{8,24},{9,... | collective-permute-start | bytes 6291464 | tf_op jit(solution)/shard_map/ppermute | solution.py:16
  793.7 44.8 %copy-start.8 = (bf16[128,512]{0,1:T(8,128)(2,1)S(1)}, bf16[128,512]{0,1:T(8,128)(2,1)}, u32[]{:S(2)}) copy-start(bf16[128,512]{0,1:T(8,128)(2,1)} %copy-done.7) | copy-start | bytes 393220
  793.7 44.8 %copy-start.19 = (f32[512]{0:T(512)S(1)}, f32[512]{0:T(512)}, u32[]{:S(2)}) copy-start(f32[512]{0:T(512)} %param.12) | copy-start | bytes 6148
where the time goes:
time: 914 us
  waiting for transfers between devices  750 us (82%)
  blocking collectives  72.7 us (8%)
  other arithmetic  35.4 us (4%)
  starting transfers between devices  22 us (2%)
  local copies, waits for them, and re-layouts  19.1 us (2%)
  matrix products  12.2 us (1%)
    ppermute x10, waiting for transfers between devices, swapped_2(): return lax.ppermute(value, axis, pairs)  750 us
    psum x1, blocking collectives, per_device(): d_skip = lax.psum(jnp.sum(grad_prod * signal, axis=0), 'ctx')  72.7 us
    ppermute x10, starting transfers between devices, swapped_2(): return lax.ppermute(value, axis, pairs)  22 us
  transfers between devices with their start and end apart: 10, of which 10 were waited for; matrix products, arithmetic and copies ran while one was open for 1% of the time, Pallas kernels for 0%

commit v1 on v0

v1 whole, which is shorter than its diff:
```python
import jax
import jax.numpy as jnp
import numpy as np
from jax import lax
from jax.experimental import pallas as pl
from jax.experimental.pallas import tpu as pltpu
from jax.sharding import PartitionSpec as P

N_DEV = 32
LOC = 128
N_FFT = 2 * N_DEV * LOC
CPD = 16
ROWS = 6 * CPD
CB = 128


def split_np(m):
    hi = np.asarray(m, np.float32).astype(jnp.bfloat16)
    lo = (np.asarray(m, np.float64) - hi.astype(np.float64)).astype(np.float32).astype(jnp.bfloat16)
    return hi, lo


def tables():
    rev = np.array([int(format(r, "05b")[::-1], 2) for r in range(N_DEV)])
    q = np.concatenate([2 * rev, 2 * rev + 1])
    d = np.arange(N_DEV)
    m = np.arange(LOC)
    ang = 2 * np.pi * (np.outer(q, d) % 64) / 64.0
    w1 = np.concatenate([np.cos(ang), -np.sin(ang)], axis=0)
    hi, lo = split_np(w1)
    w1c = np.concatenate([hi, hi, lo], axis=1)
    w2 = np.concatenate([np.cos(ang).T, -np.sin(ang).T], axis=1) / N_FFT
    hi, lo = split_np(w2)
    w2c = np.concatenate([hi, hi, lo], axis=1)
    tw = 2 * np.pi * np.outer(q, m) / N_FFT
    tc = np.tile(np.cos(tw), (1, 2)).astype(np.float32)
    ts = np.tile(np.sin(tw), (1, 2)).astype(np.float32)
    bm = 2 * np.pi * (np.outer(m, m) % LOC) / LOC
    c, s = np.cos(bm), np.sin(bm)
    fwd = np.concatenate([np.concatenate([c, -s], 1), np.concatenate([s, c], 1)], 0)
    inv = np.concatenate([np.concatenate([c, s], 1), np.concatenate([-s, c], 1)], 0)
    return (w1c, w2c, tc, ts, *split_np(fwd), *split_np(inv))


def split(v):
    hi = v.astype(jnp.bfloat16)
    lo = (v - hi.astype(jnp.float32)).astype(jnp.bfloat16)
    return hi, lo


def dot(a, b):
    return jnp.dot(a, b, preferred_element_type=jnp.float32)


def pre_kernel(x1, x2, v, go, f, out, ds):
    g = go[...].astype(jnp.float32) * x2[...].astype(jnp.float32)
    z = x1[...].astype(jnp.float32) * v[...].astype(jnp.float32)
    ds[...] = jnp.sum(g * z, axis=0, keepdims=True)
    n = CB // CPD
    out[:, 0:CPD, :] = g.T.reshape(n, CPD, LOC)
    out[:, CPD : 2 * CPD, :] = z.T.reshape(n, CPD, LOC)
    for k in range(4):
        o = (2 + k) * CPD
        out[:, o : o + CPD, :] = f[k // 2, k % 2, 0].T.reshape(n, CPD, LOC)


def rows_of(ref, row):
    return ref[pl.ds(row, N_DEV, stride=ROWS), :]


def mid_kernel(r, w1, w2, tc, ts, fh, fl, ih, il, s, bh, bl, fs):
    def put(row, val):
        s[pl.ds(row, N_DEV, stride=ROWS), :] = val

    def stage(row, val):
        hi, lo = split(val)
        bh[row : row + 64, :] = hi
        bl[row : row + 64, :] = lo

    def big(mh, ml):
        a = bh[...]
        fs[...] = dot(a, mh[...]) + dot(bl[...], mh[...]) + dot(a, ml[...])

    for c in range(CPD):
        x = jnp.concatenate([rows_of(r, c), rows_of(r, CPD + c)], axis=1)
        hi, lo = split(x)
        a = dot(w1[...], jnp.concatenate([hi, lo, hi], axis=0))
        re, im = a[:64], a[64:]
        bre = re * tc[...] + im * ts[...]
        bim = im * tc[...] - re * ts[...]
        stage(c * 128, jnp.concatenate([bre[:, :LOC], bim[:, :LOC]], axis=1))
        stage(c * 128 + 64, jnp.concatenate([bre[:, LOC:], bim[:, LOC:]], axis=1))
    big(fh, fl)
    for c in range(CPD):
        gre = fs[c * 128 : c * 128 + 64, :LOC]
        gim = fs[c * 128 : c * 128 + 64, LOC:]
        zre = fs[c * 128 + 64 : c * 128 + 128, :LOC]
        zim = fs[c * 128 + 64 : c * 128 + 128, LOC:]
        hre = jnp.concatenate([rows_of(r, 2 * CPD + c), rows_of(r, 3 * CPD + c)], axis=0)
        him = jnp.concatenate([rows_of(r, 4 * CPD + c), rows_of(r, 5 * CPD + c)], axis=0)
        dre = (zre * gre + zim * gim) * (1.0 / N_FFT)
        dim = (zre * gim - zim * gre) * (1.0 / N_FFT)
        put(2 * CPD + c, dre[:32])
        put(3 * CPD + c, dre[32:])
        put(4 * CPD + c, dim[:32])
        put(5 * CPD + c, dim[32:])
        stage(c * 128, jnp.concatenate([hre * gre + him * gim, hre * gim - him * gre], axis=1))
        stage(c * 128 + 64, jnp.concatenate([hre * zre - him * zim, hre * zim + him * zre], axis=1))
    big(ih, il)
    for c in range(CPD):
        a = fs[c * 128 : c * 128 + 64, :]
        b = fs[c * 128 + 64 : c * 128 + 128, :]
        re = jnp.concatenate([a[:, :LOC], b[:, :LOC]], axis=1)
        im = jnp.concatenate([a[:, LOC:], b[:, LOC:]], axis=1)
        ure = re * tc[...] - im * ts[...]
        uim = im * tc[...] + re * ts[...]
        hi, lo = split(jnp.concatenate([ure, uim], axis=0))
        o = dot(w2[...], jnp.concatenate([hi, lo, hi], axis=0))
        put(c, o[:, :LOC])
        put(CPD + c, o[:, LOC:])


def post_kernel(r, x1, x2, v, go, sg, d1, d2, dv, df):
    def back(k):
        return r[:, k * CPD : (k + 1) * CPD, :].reshape(CB, LOC).T

    f32 = jnp.float32
    x1f, x2f, vf, gof = (t[...].astype(f32) for t in (x1, x2, v, go))
    gain = sg[...]
    dz = back(0) + gain * (gof * x2f)
    d1[...] = (dz * vf).astype(jnp.bfloat16)
    dv[...] = (dz * x1f).astype(jnp.bfloat16)
    d2[...] = (gof * (back(1) + gain * (x1f * vf))).astype(jnp.bfloat16)
    for k in range(4):
        df[k // 2, k % 2, 0] = back(2 + k)


def per_device(x_one, x_two, values, grad_out, filter_spectrum, skip_gain):
    ch = x_one.shape[1]
    f32 = jnp.float32
    steps = ch // CB
    tab = [jnp.asarray(t) for t in tables()]
    row_spec = pl.BlockSpec((LOC, CB), lambda i: (0, i))
    filt_spec = pl.BlockSpec((2, 2, 1, LOC, CB), lambda i: (0, 0, 0, 0, i))
    pack_spec = pl.BlockSpec((CB // CPD, ROWS, LOC), lambda i: (i, 0, 0))
    vec_spec = pl.BlockSpec((1, CB), lambda i: (0, i))
    packed = jax.ShapeDtypeStruct((N_DEV, ROWS, LOC), f32)
    send, part = pl.pallas_call(
        pre_kernel,
        grid=(steps,),
        in_specs=[row_spec] * 4 + [filt_spec],
        out_specs=[pack_spec, vec_spec],
        out_shape=[packed, jax.ShapeDtypeStruct((1, ch), f32)],
        name="pre",
    )(x_one, x_two, values, grad_out, filter_spectrum)
    d_skip = lax.psum(part[0], "ctx")
    recv = lax.all_to_all(send, "ctx", 0, 0, tiled=True)
    sent = pl.pallas_call(
        mid_kernel,
        out_shape=jax.ShapeDtypeStruct((N_DEV * ROWS, LOC), f32),
        scratch_shapes=[
            pltpu.VMEM((CPD * 128, 256), jnp.bfloat16),
            pltpu.VMEM((CPD * 128, 256), jnp.bfloat16),
            pltpu.VMEM((CPD * 128, 256), f32),
        ],
        name="mid",
    )(recv.reshape(N_DEV * ROWS, LOC), *tab)
    out = lax.all_to_all(sent.reshape(N_DEV, ROWS, LOC), "ctx", 0, 0, tiled=True)
    act = jax.ShapeDtypeStruct((LOC, ch), jnp.bfloat16)
    d_one, d_two, d_values, d_filter = pl.pallas_call(
        post_kernel,
        grid=(steps,),
        in_specs=[pack_spec] + [row_spec] * 4 + [vec_spec],
        out_specs=[row_spec] * 3 + [filt_spec],
        out_shape=[act, act, act, jax.ShapeDtypeStruct(filter_spectrum.shape, f32)],
        name="post",
    )(out, x_one, x_two, values, grad_out, skip_gain[None, :])
    return d_one, d_two, d_values, d_filter, d_skip


def solution(mesh):
    act = P("ctx", "chan")
    filt = P(None, None, "ctx", None, "chan")
    return jax.shard_map(
        per_device,
        mesh=mesh,
        in_specs=(act, act, act, act, filt, P("chan")),
        out_specs=(act, act, act, filt, P("chan")),
        check_vma=False,
    )
```

time: 914 us -> 176 us (0.19)
  waiting for transfers between devices: 750 us -> 0.01 us
  blocking collectives: 72.7 us -> 152 us
  other arithmetic: 35.4 us -> 0 us
  local copies, waits for them, and re-layouts: 19.1 us -> 1.17 us
  starting transfers between devices: 22 us -> 5.76 us
  Pallas kernels: 0 us -> 16 us
  matrix products: 12.2 us -> 0 us
    ppermute x10 -> x0, waiting for transfers between devices: 750 us -> none  [swapped_2(): return lax.ppermute(value, axis, pairs)]
    all_to_all x0 -> x1, blocking collectives: none -> 50.7 us  [per_device(): recv = lax.all_to_all(send, 'ctx', 0, 0, tiled=True)]
    psum x1, blocking collectives: 72.7 us -> 101 us  [per_device(): d_skip = lax.psum(part[0], 'ctx')]
    ppermute x10 -> x0, starting transfers between devices: 22 us -> none  [swapped_2(): return lax.ppermute(value, axis, pairs)]
    select_n x9 -> x0, other arithmetic: 21.8 us -> none  [the longest x4 12.4 us: butterfly_forward(): imag_part = jnp.where(is_upper, upper_im, imag_part + other_im)]
    pallas_call x0 -> x3, Pallas kernels: none -> 16 us  [the longest x1 8.18 us: per_device(): pl.pallas_call(mid_kernel, out_shape=jax.ShapeDtypeStruct((N_DEV * ROWS,...]
    unnamed x52 -> x4, local copies, waits for them, and re-layouts: 16.3 us -> 1.17 us
    dot_general x8 -> x0, matrix products: 12.2 us -> none  [the longest x1 1.73 us: per_device(): jnp.einsum('bm,kmc->kbc', big_cos, spec_re, precision=PRECISE)]
  transfers between devices with their start and end apart: 10 -> 1, of which waited for: 10 -> 0; matrix products, arithmetic and copies ran while one was open for 1% -> 0% of each run, Pallas kernels for 0% -> 0%
where the time goes in v1:
time: 176 us; the launch traced here: 175 us
  blocking collectives  152 us (86%)
  Pallas kernels  16 us (9%)
  starting transfers between devices  5.76 us (3%)
    psum x1, blocking collectives, per_device(): d_skip = lax.psum(part[0], 'ctx')  101 us
    all_to_all x1, blocking collectives, per_device(): recv = lax.all_to_all(send, 'ctx', 0, 0, tiled=True)  50.7 us
    pallas_call x1, Pallas kernels, per_device(): pl.pallas_call(mid_kernel, out_shape=jax.ShapeDtypeStruct((N_DEV * ROWS,...  8.18 us
    all_to_all x1, starting transfers between devices, per_device(): lax.all_to_all(sent.reshape(N_DEV, ROWS, LOC), 'ctx', 0, 0, tiled=True)  5.76 us
    pallas_call x1, Pallas kernels, per_device(): pl.pallas_call(pre_kernel, grid=(steps,), in_specs=[row_spec] * 4 + [filt...  3.99 us
    pallas_call x1, Pallas kernels, per_device(): pl.pallas_call(post_kernel, grid=(steps,), in_specs=[pack_spec] + [row_sp...  3.87 us
  transfers between devices with their start and end apart: 1, of which 0 were waited for; matrix products, arithmetic and copies ran while one was open for 0% of the time, Pallas kernels for 0%

profile of v1, /device:TPU:16, one launch (start us, length us, event | category | flops | bytes accessed | tf_op | source)
XLA Modules:
  0.0 175.2 jit_solution(795338893867859397)
XLA Ops:
  0.6 4.0 %pre.1 = (f32[32,96,128]{2,1,0:T(8,128)}, f32[1,512]{1,0:T(1,128)}) custom-call(bf16[128,512]{1,0:T(8,128)(2,1)} %x1.3, bf16[128,512]{1,0:T(8,128)(2,1)} %x2.3, bf16[128,512]{1,0:T(8,128)(2,1)} %v.3, bf16[128,512]{1,0:T(8,128)(2,1)} %go.3, f32[2,2,1,128,512]{4,3,2,1,0:T(8,128)} %f.1), custom_call_target="tpu_custom_call" | custom-call | tf_op jit(solution)/shard_map/pre/pallas_call | solution.py:148
  4.6 50.7 %all_to_all.10 = f32[32,96,128]{2,1,0:T(8,128)} all-to-all(f32[32,96,128]{2,1,0:T(8,128)} %get-tuple-element.11), channel_id=1, replica_groups=mesh['chan'=8,'ctx'=32] {'ctx'}, dimensions={0} | all-to-all | bytes 3145728 | tf_op jit(solution)/shard_map/all_to_all | solution.py:157
  55.4 8.2 %mid.1 = f32[3072,128]{1,0:T(8,128)} custom-call(f32[3072,128]{1,0:T(8,128)} %bitcast.5, bf16[128,96]{1,0:T(8,128)(2,1)} %constant.16.clone.w1, bf16[32,384]{1,0:T(8,128)(2,1)} %constant.17.clone.w2, f32[64,256]{1,0:T(8,128)} %constant.18.clone.tc, f32[64,256]{1,0:T(8,128)} %constant.19.clone.ts, bf16[256,256]{1,0:T(8,128)(2,1)} %constant.20.clone.fh, ...), custom_call_target="tpu_custom_call" | custom-call | tf_op jit(solution)/shard_map/mid/pallas_call | solution.py:158
  63.5 0.0 copy-start.1
  63.5 5.8 %all-to-all-start.1 = ((f32[32,96,128]{2,1,0:T(8,128)}), f32[32,96,128]{2,1,0:T(8,128)S(1)}, u32[]{:S(2)}, u32[]{:S(2)}) async-start(f32[32,96,128]{2,1,0:T(8,128)} %bitcast.4), calls=%async_computation.1 | async-start | bytes 3145728 | tf_op jit(solution)/shard_map/all_to_all | solution.py:168
  69.3 0.0 copy-done.1
  69.3 100.9 %psum.7 = f32[512]{0:T(512)} all-reduce(f32[512]{0:T(512)S(1)} %bitcast.7), channel_id=1, replica_groups=mesh['chan'=8,'ctx'=32] {'ctx'}, use_global_device_ids=true, to_apply=%region_0.0 | all-reduce | flops 512 | bytes 4096 | tf_op jit(solution)/shard_map/psum | solution.py:156
  170.2 0.0 all-to-all-done.1.r
  170.2 0.0 copy-start
  170.2 1.2 copy-done
  171.4 3.9 %post.1 = (bf16[128,512]{1,0:T(8,128)(2,1)}, bf16[128,512]{1,0:T(8,128)(2,1)}, bf16[128,512]{1,0:T(8,128)(2,1)}, f32[2,2,1,128,512]{4,3,2,1,0:T(8,128)}) custom-call(f32[32,96,128]{2,1,0:T(8,128)} %copy-done, bf16[128,512]{1,0:T(8,128)(2,1)} %x1.3, bf16[128,512]{1,0:T(8,128)(2,1)} %x2.3, bf16[128,512]{1,0:T(8,128)(2,1)} %v.3, bf16[128,512]{1,0:T(8,128)(2,1)} %go.3, ...), custom_call_target="tpu_custom_call" | custom-call | tf_op jit(solution)/shard_map/post/pallas_call | solution.py:170
Async XLA Ops:
  63.5 5.8 %copy-start.1 = (f32[1,512]{1,0:T(1,128)S(1)}, f32[1,512]{1,0:T(1,128)}, u32[]{:S(2)}) copy-start(f32[1,512]{1,0:T(1,128)} %get-tuple-element.16) | copy-start | bytes 6148
  63.5 106.7 %all-to-all-start.1 = ((f32[32,96,128]{2,1,0:T(8,128)}), f32[32,96,128]{2,1,0:T(8,128)S(1)}, u32[]{:S(2)}, u32[]{:S(2)}) async-start(f32[32,96,128]{2,1,0:T(8,128)} %bitcast.4), calls=%async_computation.1 | async-start | bytes 3145728 | tf_op jit(solution)/shard_map/all_to_all | solution.py:168
  170.2 1.2 copy-start

commit v2 on v1

--- a/solution.py
+++ b/solution.py
@@ -11,6 +11,7 @@
 N_FFT = 2 * N_DEV * LOC
 CPD = 16
 ROWS = 6 * CPD
+ROWS_OUT = ROWS + 8
 CB = 128
 
 
@@ -52,10 +53,9 @@
     return jnp.dot(a, b, preferred_element_type=jnp.float32)
 
 
-def pre_kernel(x1, x2, v, go, f, out, ds):
+def pre_kernel(x1, x2, v, go, f, out):
     g = go[...].astype(jnp.float32) * x2[...].astype(jnp.float32)
     z = x1[...].astype(jnp.float32) * v[...].astype(jnp.float32)
-    ds[...] = jnp.sum(g * z, axis=0, keepdims=True)
     n = CB // CPD
     out[:, 0:CPD, :] = g.T.reshape(n, CPD, LOC)
     out[:, CPD : 2 * CPD, :] = z.T.reshape(n, CPD, LOC)
@@ -70,7 +70,7 @@
 
 def mid_kernel(r, w1, w2, tc, ts, fh, fl, ih, il, s, bh, bl, fs):
     def put(row, val):
-        s[pl.ds(row, N_DEV, stride=ROWS), :] = val
+        s[pl.ds(row, N_DEV, stride=ROWS_OUT), :] = val
 
     def stage(row, val):
         hi, lo = split(val)
@@ -81,8 +81,10 @@
         a = bh[...]
         fs[...] = dot(a, mh[...]) + dot(bl[...], mh[...]) + dot(a, ml[...])
 
+    sums = []
     for c in range(CPD):
         x = jnp.concatenate([rows_of(r, c), rows_of(r, CPD + c)], axis=1)
+        sums.append(jnp.sum(x[:, :LOC] * x[:, LOC:], axis=0, keepdims=True))
         hi, lo = split(x)
         a = dot(w1[...], jnp.concatenate([hi, lo, hi], axis=0))
         re, im = a[:64], a[64:]
@@ -90,6 +92,14 @@
         bim = im * tc[...] - re * ts[...]
         stage(c * 128, jnp.concatenate([bre[:, :LOC], bim[:, :LOC]], axis=1))
         stage(c * 128 + 64, jnp.concatenate([bre[:, LOC:], bim[:, LOC:]], axis=1))
+    tot = jnp.sum(jnp.concatenate(sums, axis=0), axis=1, keepdims=True)
+    lane = lax.broadcasted_iota(jnp.int32, (CPD, LOC), 1)
+    row = lax.broadcasted_iota(jnp.int32, (CPD, LOC), 0)
+    place = lax.axis_index("ctx") % (CB // CPD) * CPD
+    mine = jnp.where(lane == place + row, jnp.broadcast_to(tot, (CPD, LOC)), 0.0)
+    skip = jnp.broadcast_to(jnp.sum(mine, axis=0, keepdims=True), (8, LOC))
+    for d in range(N_DEV):
+        s[d * ROWS_OUT + ROWS : d * ROWS_OUT + ROWS + 8, :] = skip
     big(fh, fl)
     for c in range(CPD):
         gre = fs[c * 128 : c * 128 + 64, :LOC]
@@ -120,7 +130,7 @@
         put(CPD + c, o[:, LOC:])
 
 
-def post_kernel(r, x1, x2, v, go, sg, d1, d2, dv, df):
+def post_kernel(r, x1, x2, v, go, sg, d1, d2, dv, df, ds):
     def back(k):
         return r[:, k * CPD : (k + 1) * CPD, :].reshape(CB, LOC).T
 
@@ -133,6 +143,7 @@
     d2[...] = (gof * (back(1) + gain * (x1f * vf))).astype(jnp.bfloat16)
     for k in range(4):
         df[k // 2, k % 2, 0] = back(2 + k)
+    ds[...] = jnp.sum(r[:, ROWS, :], axis=0, keepdims=True)
 
 
 def per_device(x_one, x_two, values, grad_out, filter_spectrum, skip_gain):
@@ -145,19 +156,18 @@
     pack_spec = pl.BlockSpec((CB // CPD, ROWS, LOC), lambda i: (i, 0, 0))
     vec_spec = pl.BlockSpec((1, CB), lambda i: (0, i))
     packed = jax.ShapeDtypeStruct((N_DEV, ROWS, LOC), f32)
-    send, part = pl.pallas_call(
+    send = pl.pallas_call(
         pre_kernel,
         grid=(steps,),
         in_specs=[row_spec] * 4 + [filt_spec],
-        out_specs=[pack_spec, vec_spec],
-        out_shape=[packed, jax.ShapeDtypeStruct((1, ch), f32)],
+        out_specs=pack_spec,
+        out_shape=packed,
         name="pre",
     )(x_one, x_two, values, grad_out, filter_spectrum)
-    d_skip = lax.psum(part[0], "ctx")
     recv = lax.all_to_all(send, "ctx", 0, 0, tiled=True)
     sent = pl.pallas_call(
         mid_kernel,
-        out_shape=jax.ShapeDtypeStruct((N_DEV * ROWS, LOC), f32),
+        out_shape=jax.ShapeDtypeStruct((N_DEV * ROWS_OUT, LOC), f32),
         scratch_shapes=[
             pltpu.VMEM((CPD * 128, 256), jnp.bfloat16),
             pltpu.VMEM((CPD * 128, 256), jnp.bfloat16),
@@ -165,17 +175,17 @@
         ],
         name="mid",
     )(recv.reshape(N_DEV * ROWS, LOC), *tab)
-    out = lax.all_to_all(sent.reshape(N_DEV, ROWS, LOC), "ctx", 0, 0, tiled=True)
+    out = lax.all_to_all(sent.reshape(N_DEV, ROWS_OUT, LOC), "ctx", 0, 0, tiled=True)
     act = jax.ShapeDtypeStruct((LOC, ch), jnp.bfloat16)
-    d_one, d_two, d_values, d_filter = pl.pallas_call(
+    d_one, d_two, d_values, d_filter, d_skip = pl.pallas_call(
         post_kernel,
         grid=(steps,),
-        in_specs=[pack_spec] + [row_spec] * 4 + [vec_spec],
-        out_specs=[row_spec] * 3 + [filt_spec],
-        out_shape=[act, act, act, jax.ShapeDtypeStruct(filter_spectrum.shape, f32)],
+        in_specs=[pl.BlockSpec((CB // CPD, ROWS_OUT, LOC), lambda i: (i, 0, 0))] + [row_spec] * 4 + [vec_spec],
+        out_specs=[row_spec] * 3 + [filt_spec, vec_spec],
+        out_shape=[act, act, act, jax.ShapeDtypeStruct(filter_spectrum.shape, f32), jax.ShapeDtypeStruct((1, ch), f32)],
         name="post",
     )(out, x_one, x_two, values, grad_out, skip_gain[None, :])
-    return d_one, d_two, d_values, d_filter, d_skip
+    return d_one, d_two, d_values, d_filter, d_skip[0]
 
 
 def solution(mesh):

time: 176 us -> 115 us (0.65)
  blocking collectives: 152 us -> 99.1 us
  starting transfers between devices: 5.76 us -> 0 us
    psum x1 -> x0, blocking collectives: 101 us -> none  [per_device(): d_skip = lax.psum(part[0], 'ctx')]
    all_to_all x0 -> x1, blocking collectives: none -> 48.4 us  [per_device(): lax.all_to_all(sent.reshape(N_DEV, ROWS_OUT, LOC), 'ctx', 0, 0, tiled=True)]
    all_to_all x1 -> x0, starting transfers between devices: 5.76 us -> none  [per_device(): lax.all_to_all(sent.reshape(N_DEV, ROWS, LOC), 'ctx', 0, 0, tiled=True)]
  transfers between devices with their start and end apart: 1 -> 0, of which waited for: 0 -> 0; matrix products, arithmetic and copies ran while one was open for 0% -> 0% of each run, Pallas kernels for 0% -> 0%
where the time goes in v2:
time: 115 us
  blocking collectives  99.1 us (86%)
  Pallas kernels  15.3 us (13%)
    all_to_all x1, blocking collectives, per_device(): recv = lax.all_to_all(send, 'ctx', 0, 0, tiled=True)  50.7 us
    all_to_all x1, blocking collectives, per_device(): lax.all_to_all(sent.reshape(N_DEV, ROWS_OUT, LOC), 'ctx', 0, 0, tiled=True)  48.4 us
    pallas_call x1, Pallas kernels, per_device(): pl.pallas_call(mid_kernel, out_shape=jax.ShapeDtypeStruct((N_DEV * ROWS_O...  7.41 us
    pallas_call x1, Pallas kernels, per_device(): pl.pallas_call(pre_kernel, grid=(steps,), in_specs=[row_spec] * 4 + [filt...  3.96 us
    pallas_call x1, Pallas kernels, per_device(): pl.pallas_call(post_kernel, grid=(steps,), in_specs=[pl.BlockSpec((CB //...  3.9 us

profile of v2, /device:TPU:16, one launch (start us, length us, event | category | flops | bytes accessed | tf_op | source)
XLA Modules:
  0.0 115.1 jit_solution(464826933203326302)
XLA Ops:
  0.6 4.0 %pre.1 = f32[32,96,128]{2,1,0:T(8,128)} custom-call(bf16[128,512]{1,0:T(8,128)(2,1)} %x1.3, bf16[128,512]{1,0:T(8,128)(2,1)} %x2.3, bf16[128,512]{1,0:T(8,128)(2,1)} %v.3, bf16[128,512]{1,0:T(8,128)(2,1)} %go.3, f32[2,2,1,128,512]{4,3,2,1,0:T(8,128)} %f.1), custom_call_target="tpu_custom_call" | custom-call | tf_op jit(solution)/shard_map/pre/pallas_call | solution.py:159
  4.6 50.7 %all_to_all.10 = f32[32,96,128]{2,1,0:T(8,128)} all-to-all(f32[32,96,128]{2,1,0:T(8,128)} %pre.1), channel_id=1, replica_groups=mesh['chan'=8,'ctx'=32] {'ctx'}, dimensions={0} | all-to-all | bytes 3145728 | tf_op jit(solution)/shard_map/all_to_all | solution.py:167
  55.3 7.4 %mid.1 = f32[3328,128]{1,0:T(8,128)} custom-call(f32[3072,128]{1,0:T(8,128)} %bitcast.5, bf16[128,96]{1,0:T(8,128)(2,1)} %constant.16.clone.w1, bf16[32,384]{1,0:T(8,128)(2,1)} %constant.17.clone.w2, f32[64,256]{1,0:T(8,128)} %constant.18.clone.tc, f32[64,256]{1,0:T(8,128)} %constant.19.clone.ts, bf16[256,256]{1,0:T(8,128)(2,1)} %constant.20.clone.fh, ...), custom_call_target="tpu_custom_call" | custom-call | tf_op jit(solution)/shard_map/mid/pallas_call | solution.py:168
  62.7 48.4 %all_to_all.11.r = f32[32,104,128]{2,1,0:T(8,128)} all-to-all(f32[32,104,128]{2,1,0:T(8,128)} %bitcast.4), channel_id=1, replica_groups=mesh['chan'=8,'ctx'=32] {'ctx'}, dimensions={0} | all-to-all | bytes 3407872 | tf_op jit(solution)/shard_map/all_to_all | solution.py:178
  111.1 3.9 %post.1 = (bf16[128,512]{1,0:T(8,128)(2,1)}, bf16[128,512]{1,0:T(8,128)(2,1)}, bf16[128,512]{1,0:T(8,128)(2,1)}, f32[2,2,1,128,512]{4,3,2,1,0:T(8,128)}, f32[1,512]{1,0:T(1,128)}) custom-call(f32[32,104,128]{2,1,0:T(8,128)} %all_to_all.11.r, bf16[128,512]{1,0:T(8,128)(2,1)} %x1.3, bf16[128,512]{1,0:T(8,128)(2,1)} %x2.3, bf16[128,512]{1,0:T(8,128)(2,1)} %v.3, ...), custom_call_target="tpu_custom_call" | custom-call | tf_op jit(solution)/shard_map/post/pallas_call | solution.py:180

commit v3 on v2

v3 whole, which is shorter than its diff:
```python
import jax
import jax.numpy as jnp
import numpy as np
from jax import lax
from jax.experimental import pallas as pl
from jax.experimental.pallas import tpu as pltpu
from jax.sharding import PartitionSpec as P

N_DEV = 32
LOC = 128
N_FFT = 2 * N_DEV * LOC
CPD = 16
CB = 128


def split_np(m):
    hi = np.asarray(m, np.float32).astype(jnp.bfloat16)
    lo = (np.asarray(m, np.float64) - hi.astype(np.float64)).astype(np.float32).astype(jnp.bfloat16)
    return hi, lo


def tables():
    rev = np.array([int(format(r, "05b")[::-1], 2) for r in range(N_DEV)])
    q = np.concatenate([2 * rev, 2 * rev + 1])
    d = np.arange(N_DEV)
    m = np.arange(LOC)
    ang = 2 * np.pi * (np.outer(q, d) % 64) / 64.0
    w1 = np.concatenate([np.cos(ang), -np.sin(ang)], axis=0)
    hi, lo = split_np(w1)
    w1c = np.concatenate([hi, hi, lo], axis=1)
    w2 = np.concatenate([np.cos(ang).T, -np.sin(ang).T], axis=1) / N_FFT
    hi, lo = split_np(w2)
    w2c = np.concatenate([hi, hi, lo], axis=1)
    tw = 2 * np.pi * np.outer(q, m) / N_FFT
    tc = np.tile(np.cos(tw), (1, 2)).astype(np.float32)
    ts = np.tile(np.sin(tw), (1, 2)).astype(np.float32)
    bm = 2 * np.pi * (np.outer(m, m) % LOC) / LOC
    c, s = np.cos(bm), np.sin(bm)
    fwd = np.concatenate([np.concatenate([c, -s], 1), np.concatenate([s, c], 1)], 0)
    inv = np.concatenate([np.concatenate([c, s], 1), np.concatenate([-s, c], 1)], 0)
    return (w1c, w2c, tc, ts, *split_np(fwd), *split_np(inv))


def split(v):
    hi = v.astype(jnp.bfloat16)
    lo = (v - hi.astype(jnp.float32)).astype(jnp.bfloat16)
    return hi, lo


def dot(a, b):
    return jnp.dot(a, b, preferred_element_type=jnp.float32)


N_Z = 8
N_X = 4


def spot():
    here = lax.axis_index("ctx")
    return here // N_Z, here % N_Z


def pre_kernel(dep, x1, x2, v, go, out):
    g = go[...].astype(jnp.float32) * x2[...].astype(jnp.float32)
    z = x1[...].astype(jnp.float32) * v[...].astype(jnp.float32)
    n = CB // CPD
    out[:, 0:CPD, :] = g.T.reshape(n, CPD, LOC)
    out[:, CPD : 2 * CPD, :] = z.T.reshape(n, CPD, LOC)


def filt_kernel(f, o0, o1, o2, o3, tmp):
    mx, mz = spot()
    for l, out in enumerate((o0, o1, o2, o3)):
        cols = pl.ds(pl.multiple_of((l ^ mx) * CB, CB), CB)
        for k in range(4):
            tmp[k] = f[k // 2, k % 2, 0, :, cols].T
        for k in range(4):
            for zz in range(N_Z):
                out[zz, k * CPD : (k + 1) * CPD, :] = tmp[k, pl.ds(pl.multiple_of((zz ^ mz) * CPD, CPD), CPD), :]


def turn_filt(dep, *refs):
    for k in range(N_Z):
        for l in range(N_X):
            refs[N_X + k][l] = refs[l][k]


def turn_out(dep, *refs):
    for k in range(N_Z):
        for l in range(N_X):
            refs[N_X + k][l * 32 : (l + 1) * 32, :] = refs[l][k * 32 : (k + 1) * 32, :]
            refs[N_X + k][128 + l : 129 + l, :] = refs[l][256:257, :]
        refs[N_X + k][132:136, :] = jnp.zeros((4, LOC), jnp.float32)


def rows_of(ref, row, rows):
    return ref[pl.ds(row, N_DEV, stride=rows), :]


def put(ref, row, rows, val):
    ref[pl.ds(row, N_DEV, stride=rows), :] = val


def stage(bh, bl, row, val):
    hi, lo = split(val)
    bh[row : row + 64, :] = hi
    bl[row : row + 64, :] = lo


def big(bh, bl, mh, ml):
    a = bh[...]
    return dot(a, mh[...]) + dot(bl[...], mh[...]) + dot(a, ml[...])


def fwd_kernel(r, w1, tc, ts, fh, fl, fs, s, sk, bh, bl):
    sums = []
    for c in range(CPD):
        x = jnp.concatenate([rows_of(r, c, 2 * CPD), rows_of(r, CPD + c, 2 * CPD)], axis=1)
        sums.append(jnp.sum(x[:, :LOC] * x[:, LOC:], axis=0, keepdims=True))
        hi, lo = split(x)
        a = dot(w1[...], jnp.concatenate([hi, lo, hi], axis=0))
        re, im = a[:64], a[64:]
        bre = re * tc[...] + im * ts[...]
        bim = im * tc[...] - re * ts[...]
        stage(bh, bl, c * 128, jnp.concatenate([bre[:, :LOC], bim[:, :LOC]], axis=1))
        stage(bh, bl, c * 128 + 64, jnp.concatenate([bre[:, LOC:], bim[:, LOC:]], axis=1))
    tot = jnp.sum(jnp.concatenate(sums, axis=0), axis=1, keepdims=True)
    lane = lax.broadcasted_iota(jnp.int32, (CPD, LOC), 1)
    row = lax.broadcasted_iota(jnp.int32, (CPD, LOC), 0)
    mine = jnp.where(lane == spot()[1] * CPD + row, jnp.broadcast_to(tot, (CPD, LOC)), 0.0)
    sk[...] = jnp.broadcast_to(jnp.sum(mine, axis=0, keepdims=True), (8, LOC))
    fs[...] = big(bh, bl, fh, fl)
    for c in range(CPD):
        gre = fs[c * 128 : c * 128 + 64, :LOC]
        gim = fs[c * 128 : c * 128 + 64, LOC:]
        zre = fs[c * 128 + 64 : c * 128 + 128, :LOC]
        zim = fs[c * 128 + 64 : c * 128 + 128, LOC:]
        dre = (zre * gre + zim * gim) * (1.0 / N_FFT)
        dim = (zre * gim - zim * gre) * (1.0 / N_FFT)
        put(s, c, 4 * CPD, dre[:32])
        put(s, CPD + c, 4 * CPD, dre[32:])
        put(s, 2 * CPD + c, 4 * CPD, dim[:32])
        put(s, 3 * CPD + c, 4 * CPD, dim[32:])


def inv_kernel(*refs):
    fs, (sk, w2, tc, ts, ih, il), srcs = refs[0], refs[1:7], refs[7 : 7 + N_Z]
    outs = refs[7 + N_Z : 7 + N_Z + N_X]
    bh, bl, ys, r, s = refs[7 + N_Z + N_X :]
    mx, mz = spot()
    for k in range(N_Z):
        for l in range(N_X):
            dev = (l ^ mx) * N_Z + (k ^ mz)
            r[pl.ds(pl.multiple_of(dev * 64, 64), 64), :] = srcs[k][l]
    for c in range(CPD):
        gre = fs[c * 128 : c * 128 + 64, :LOC]
        gim = fs[c * 128 : c * 128 + 64, LOC:]
        zre = fs[c * 128 + 64 : c * 128 + 128, :LOC]
        zim = fs[c * 128 + 64 : c * 128 + 128, LOC:]
        hre = jnp.concatenate([rows_of(r, c, 4 * CPD), rows_of(r, CPD + c, 4 * CPD)], axis=0)
        him = jnp.concatenate([rows_of(r, 2 * CPD + c, 4 * CPD), rows_of(r, 3 * CPD + c, 4 * CPD)], axis=0)
        stage(bh, bl, c * 128, jnp.concatenate([hre * gre + him * gim, hre * gim - him * gre], axis=1))
        stage(bh, bl, c * 128 + 64, jnp.concatenate([hre * zre - him * zim, hre * zim + him * zre], axis=1))
    ys[...] = big(bh, bl, ih, il)
    for c in range(CPD):
        a = ys[c * 128 : c * 128 + 64, :]
        b = ys[c * 128 + 64 : c * 128 + 128, :]
        re = jnp.concatenate([a[:, :LOC], b[:, :LOC]], axis=1)
        im = jnp.concatenate([a[:, LOC:], b[:, LOC:]], axis=1)
        ure = re * tc[...] - im * ts[...]
        uim = im * tc[...] + re * ts[...]
        hi, lo = split(jnp.concatenate([ure, uim], axis=0))
        o = dot(w2[...], jnp.concatenate([hi, lo, hi], axis=0))
        put(s, c, 2 * CPD, o[:, :LOC])
        put(s, CPD + c, 2 * CPD, o[:, LOC:])
    for l in range(N_X):
        for k in range(N_Z):
            dev = (l ^ mx) * N_Z + (k ^ mz)
            outs[l][k * 32 : (k + 1) * 32, :] = s[pl.ds(pl.multiple_of(dev * 32, 32), 32), :]
        outs[l][256:264, :] = sk[...]


def post_kernel(*refs):
    srcs, (x1, x2, v, go, sg, d1, d2, dv, ds, tmp) = refs[:N_Z], refs[N_Z:]
    f32 = jnp.float32
    mx, mz = spot()
    for l in range(N_X):
        cols = pl.ds(pl.multiple_of((l ^ mx) * CB, CB), CB)
        skip = srcs[0][128 + l : 129 + l, :]
        for k in range(N_Z):
            if k:
                skip = skip + srcs[k][128 + l : 129 + l, :]
            at = pl.ds(pl.multiple_of((k ^ mz) * CPD, CPD), CPD)
            tmp[0, at, :] = srcs[k][l * 32 : l * 32 + CPD, :]
            tmp[1, at, :] = srcs[k][l * 32 + CPD : (l + 1) * 32, :]
        ds[:, cols] = skip
        x1f, x2f, vf, gof = (t[:, cols].astype(f32) for t in (x1, x2, v, go))
        gain = sg[:, cols]
        dz = tmp[0].T + gain * (gof * x2f)
        d1[:, cols] = (dz * vf).astype(jnp.bfloat16)
        dv[:, cols] = (dz * x1f).astype(jnp.bfloat16)
        d2[:, cols] = (gof * (tmp[1].T + gain * (x1f * vf))).astype(jnp.bfloat16)


def dfilt_kernel(r, df):
    for k in range(4):
        df[k // 2, k % 2, 0] = r[:, k * CPD : (k + 1) * CPD, :].reshape(CB, LOC).T


def per_device(x_one, x_two, values, grad_out, filter_spectrum, skip_gain):
    ch = x_one.shape[1]
    f32 = jnp.float32
    bf16 = jnp.bfloat16
    steps = ch // CB
    w1, w2, tc, ts, fh, fl, ih, il = [jnp.asarray(t) for t in tables()]
    any_ = pl.BlockSpec(memory_space=pl.ANY)
    vmem = pl.BlockSpec(memory_space=pltpu.VMEM)
    row_spec = pl.BlockSpec((LOC, CB), lambda i: (0, i))
    filt_spec = pl.BlockSpec((2, 2, 1, LOC, CB), lambda i: (0, 0, 0, 0, i))

    def shape(*dims):
        return jax.ShapeDtypeStruct(dims, f32)

    def pack_spec(k):
        return pl.BlockSpec((CB // CPD, k * CPD, LOC), lambda i: (i, 0, 0))

    def exchange(v):
        return lax.all_to_all(v.reshape(N_DEV, -1, LOC), "ctx", 0, 0, tiled=True)

    def hops(vs, step, order):
        out = list(vs)
        for k in order:
            out[k] = lax.ppermute(vs[k], "ctx", [(d, d ^ (k * step)) for d in range(N_DEV)])
        return out

    x_order = (2, 1, 3)
    z_order = (4, 3, 5, 2, 6, 1, 7)
    half = pltpu.VMEM((CPD * 128, 256), bf16)
    whole = pltpu.VMEM((CPD * 128, 256), f32)
    hx = pl.pallas_call(
        filt_kernel,
        out_shape=[shape(N_Z, 64, LOC)] * N_X,
        scratch_shapes=[pltpu.VMEM((4, LOC, LOC), f32)],
        name="filt",
    )(filter_spectrum)
    s1 = pl.pallas_call(
        pre_kernel,
        grid=(steps,),
        in_specs=[any_] + [row_spec] * 4,
        out_specs=pack_spec(2),
        out_shape=shape(N_DEV, 2 * CPD, LOC),
        name="pre",
    )(hx[0], x_one, x_two, values, grad_out)
    hx = hops(hx, N_Z, x_order)
    r1 = exchange(s1)
    hz = pl.pallas_call(
        turn_filt,
        in_specs=[any_] + [vmem] * N_X,
        out_shape=[shape(N_X, 64, LOC)] * N_Z,
        name="turn_filt",
    )(s1, *hx)
    hz = hops(hz, 1, z_order)
    fs, s3, sk = pl.pallas_call(
        fwd_kernel,
        out_shape=[shape(CPD * 128, 256), shape(N_DEV * 64, LOC), shape(8, LOC)],
        scratch_shapes=[half, half],
        name="fwd",
    )(r1.reshape(-1, LOC), w1, tc, ts, fh, fl)
    r3 = exchange(s3)
    ox = pl.pallas_call(
        inv_kernel,
        out_shape=[shape(264, LOC)] * N_X,
        scratch_shapes=[
            half,
            half,
            whole,
            pltpu.VMEM((N_DEV * 64, LOC), f32),
            pltpu.VMEM((N_DEV * 32, LOC), f32),
        ],
        name="inv",
    )(fs, sk, w2, tc, ts, ih, il, *hz)
    ox = hops(ox, N_Z, x_order)
    oz = pl.pallas_call(
        turn_out,
        in_specs=[any_] + [vmem] * N_X,
        out_shape=[shape(136, LOC)] * N_Z,
        name="turn_out",
    )(sk, *ox)
    oz = hops(oz, 1, z_order)
    d_filter = pl.pallas_call(
        dfilt_kernel,
        grid=(steps,),
        in_specs=[pack_spec(4)],
        out_specs=filt_spec,
        out_shape=shape(*filter_spectrum.shape),
        name="dfilt",
    )(r3)
    act = jax.ShapeDtypeStruct((LOC, ch), bf16)
    d_one, d_two, d_values, d_skip = pl.pallas_call(
        post_kernel,
        out_shape=[act, act, act, shape(1, ch)],
        scratch_shapes=[pltpu.VMEM((2, LOC, LOC), f32)],
        name="post",
    )(*oz, x_one, x_two, values, grad_out, skip_gain[None, :])
    return d_one, d_two, d_values, d_filter, d_skip[0]


def solution(mesh):
    act = P("ctx", "chan")
    filt = P(None, None, "ctx", None, "chan")

    return jax.shard_map(
        per_device,
        mesh=mesh,
        in_specs=(act, act, act, act, filt, P("chan")),
        out_specs=(act, act, act, filt, P("chan")),
        check_vma=False,
    )
```

time: 115 us -> 156 us (1.36)
  blocking collectives: 99.1 us -> 28.3 us
  waiting for transfers between devices: 0 us -> 50.6 us
  starting transfers between devices: 0 us -> 45 us
  Pallas kernels: 15.3 us -> 26.3 us
  local copies, waits for them, and re-layouts: 0 us -> 3.59 us
    all_to_all x2 -> x1, blocking collectives: 99.1 us -> 28.3 us  [exchange(): return lax.all_to_all(v.reshape(N_DEV, -1, LOC), 'ctx', 0, 0, tiled=True)]
    ppermute x0 -> x20, waiting for transfers between devices: none -> 50.6 us  [hops(): lax.ppermute(vs[k], 'ctx', [(d, d ^ k * step) for d in range(N_DEV)])]
    ppermute x0 -> x20, starting transfers between devices: none -> 39.2 us  [hops(): lax.ppermute(vs[k], 'ctx', [(d, d ^ k * step) for d in range(N_DEV)])]
    pallas_call x3 -> x8, Pallas kernels: 15.3 us -> 26.3 us  [the longest x1 5.54 us: per_device(): pl.pallas_call(inv_kernel, out_shape=[shape(264, LOC)] * N_X, scratch_sha...]
    all_to_all x0 -> x1, starting transfers between devices: none -> 5.77 us  [exchange(): return lax.all_to_all(v.reshape(N_DEV, -1, LOC), 'ctx', 0, 0, tiled=True)]
    unnamed x0 -> x48, local copies, waits for them, and re-layouts: none -> 3.59 us
  transfers between devices with their start and end apart: 0 -> 21, of which waited for: 0 -> 13; matrix products, arithmetic and copies ran while one was open for 0% -> 0% of each run, Pallas kernels for 0% -> 8%
where the time goes in v3:
time: 156 us; the launch traced here: 155 us
  waiting for transfers between devices  50.6 us (32%)
  starting transfers between devices  45 us (29%)
  blocking collectives  28.3 us (18%)
  Pallas kernels  26.3 us (17%)
  local copies, waits for them, and re-layouts  3.59 us (2%)
    ppermute x20, waiting for transfers between devices, hops(): lax.ppermute(vs[k], 'ctx', [(d, d ^ k * step) for d in range(N_DEV)])  50.6 us
    ppermute x20, starting transfers between devices, hops(): lax.ppermute(vs[k], 'ctx', [(d, d ^ k * step) for d in range(N_DEV)])  39.2 us
    all_to_all x1, blocking collectives, exchange(): return lax.all_to_all(v.reshape(N_DEV, -1, LOC), 'ctx', 0, 0, tiled=True)  28.3 us
    all_to_all x1, starting transfers between devices, exchange(): return lax.all_to_all(v.reshape(N_DEV, -1, LOC), 'ctx', 0, 0, tiled=True)  5.77 us
    pallas_call x1, Pallas kernels, per_device(): pl.pallas_call(inv_kernel, out_shape=[shape(264, LOC)] * N_X, scratch_sha...  5.54 us
    pallas_call x1, Pallas kernels, per_device(): pl.pallas_call(fwd_kernel, out_shape=[shape(CPD * 128, 256), shape(N_DEV...  5.38 us
    pallas_call x1, Pallas kernels, per_device(): pl.pallas_call(dfilt_kernel, grid=(steps,), in_specs=[pack_spec(4)], out_...  3.59 us
    unnamed x48, local copies, waits for them, and re-layouts  3.59 us
  transfers between devices with their start and end apart: 21, of which 13 were waited for; matrix products, arithmetic and copies ran while one was open for 0% of the time, Pallas kernels for 8%

profile of v3, /device:TPU:16, one launch (start us, length us, event | category | flops | bytes accessed | tf_op | source)
XLA Modules:
  0.0 154.6 jit_solution(8887040060772531249)
XLA Ops:
  0.6 2.4 %filt.1 = (f32[8,64,128]{2,1,0:T(8,128)}, f32[8,64,128]{2,1,0:T(8,128)}, f32[8,64,128]{2,1,0:T(8,128)}, f32[8,64,128]{2,1,0:T(8,128)}) custom-call(f32[2,2,1,128,512]{4,3,2,1,0:T(8,128)} %f.1), custom_call_target="tpu_custom_call" | custom-call | tf_op jit(solution)/shard_map/filt/pallas_call | solution.py:240
  3.0 3.1 %pre.1.dep = f32[32,32,128]{2,1,0:T(8,128)} custom-call(f32[8,64,128]{2,1,0:T(8,128)} %get-tuple-element.36.dep.refs_0_, bf16[128,512]{1,0:T(8,128)(2,1)} %refs_8_.1, bf16[128,512]{1,0:T(8,128)(2,1)} %refs_9_.1, bf16[128,512]{1,0:T(8,128)(2,1)} %refs_10_.1, bf16[128,512]{1,0:T(8,128)(2,1)} %refs_11_.1), custom_call_target="tpu_custom_call" | custom-call | tf_op jit(solution)/shard_map/pre/pallas_call | solution.py:246
  6.2 28.3 %all_to_all.10 = f32[32,32,128]{2,1,0:T(8,128)} all-to-all(f32[32,32,128]{2,1,0:T(8,128)} %pre.1.dep), channel_id=1, replica_groups=mesh['chan'=8,'ctx'=32] {'ctx'}, dimensions={0} | all-to-all | bytes 1048576 | tf_op jit(solution)/shard_map/all_to_all | solution.py:228
  34.4 5.4 %fwd.1 = (f32[2048,256]{1,0:T(8,128)}, f32[2048,128]{1,0:T(8,128)}, f32[8,128]{1,0:T(8,128)}) custom-call(f32[1024,128]{1,0:T(8,128)} %bitcast.4, bf16[128,96]{1,0:T(8,128)(2,1)} %constant.16.clone.w1, f32[64,256]{1,0:T(8,128)} %constant.18.clone.tc.refs_3_, f32[64,256]{1,0:T(8,128)} %constant.19.clone.ts.refs_4_, bf16[256,256]{1,0:T(8,128)(2,1)} %constant.20.clone.fh, ...), custom_call_target="tpu_custom_call" | custom-call | tf_op jit(solution)/shard_map/fwd/pallas_call | solution.py:263
  39.8 5.8 %all-to-all-start.1 = ((f32[32,64,128]{2,1,0:T(8,128)}), f32[32,64,128]{2,1,0:T(8,128)S(1)}, u32[]{:S(2)}, u32[]{:S(2)}) async-start(f32[32,64,128]{2,1,0:T(8,128)} %bitcast.5), calls=%async_computation.1 | async-start | bytes 2097152 | tf_op jit(solution)/shard_map/all_to_all | solution.py:228
  45.6 1.9 %collective-permute-start = (f32[8,64,128]{2,1,0:T(8,128)S(1)}, f32[8,64,128]{2,1,0:T(8,128)S(1)}, u32[]{:S(2)}, u32[]{:S(2)}) collective-permute-start(f32[8,64,128]{2,1,0:T(8,128)S(1)} %copy-done.23), channel_id=1, source_target_pairs={{0,8},{1,9},{2,10},{3,11},{4,12},{5,13},{6,14},{7,15},{8,0},{9,1},... | collective-permute-start | bytes 786440 | tf_op jit(solution)/shard_map/ppermute | solution.py:233
  47.5 2.7 %collective-permute-start.1 = (f32[8,64,128]{2,1,0:T(8,128)S(1)}, f32[8,64,128]{2,1,0:T(8,128)S(1)}, u32[]{:S(2)}, u32[]{:S(2)}) collective-permute-start(f32[8,64,128]{2,1,0:T(8,128)S(1)} %copy-done.22), channel_id=1, source_target_pairs={{0,16},{1,17},{2,18},{3,19},{4,20},{5,21},{6,22},{7,23},{8,24},{9,... | collective-permute-start | bytes 786440 | tf_op jit(solution)/shard_map/ppermute | solution.py:233
  50.2 0.2 collective-permute-start.2
  50.4 10.6 %collective-permute-done.refs_1_ = f32[8,64,128]{2,1,0:T(8,128)S(1)} collective-permute-done((f32[8,64,128]{2,1,0:T(8,128)S(1)}, f32[8,64,128]{2,1,0:T(8,128)S(1)}, u32[]{:S(2)}, u32[]{:S(2)}) %collective-permute-start) | collective-permute-done | bytes 262176 | tf_op jit(solution)/shard_map/ppermute | solution.py:233
  61.0 9.5 %collective-permute-done.1.refs_2_ = f32[8,64,128]{2,1,0:T(8,128)S(1)} collective-permute-done((f32[8,64,128]{2,1,0:T(8,128)S(1)}, f32[8,64,128]{2,1,0:T(8,128)S(1)}, u32[]{:S(2)}, u32[]{:S(2)}) %collective-permute-start.1) | collective-permute-done | bytes 262176 | tf_op jit(solution)/shard_map/ppermute | solution.py:233
  70.4 1.7 %collective-permute-done.2.refs_3_ = f32[8,64,128]{2,1,0:T(8,128)S(1)} collective-permute-done((f32[8,64,128]{2,1,0:T(8,128)S(1)}, f32[8,64,128]{2,1,0:T(8,128)S(1)}, u32[]{:S(2)}, u32[]{:S(2)}) %collective-permute-start.2) | collective-permute-done | bytes 262176 | tf_op jit(solution)/shard_map/ppermute | solution.py:233
  72.1 0.7 copy-done.3
  72.8 2.2 %turn_filt.1 = (f32[4,64,128]{2,1,0:T(8,128)}, f32[4,64,128]{2,1,0:T(8,128)}, f32[4,64,128]{2,1,0:T(8,128)}, f32[4,64,128]{2,1,0:T(8,128)}, f32[4,64,128]{2,1,0:...) custom-call(f32[32,32,128]{2,1,0:T(8,128)} %pre.1.dep, ...), custom_call_target="tpu_custom_call" | custom-call | tf_op jit(solution)/shard_map/turn_filt/pallas_call | solution.py:256
  75.0 0.4 collective-permute-start.3
  75.4 3.2 %collective-permute-start.4 = (f32[4,64,128]{2,1,0:T(8,128)}, f32[4,64,128]{2,1,0:T(8,128)S(1)}, u32[]{:S(2)}, u32[]{:S(2)}) collective-permute-start(f32[4,64,128]{2,1,0:T(8,128)} %get-tuple-element.44), channel_id=1, source_target_pairs={{0,2},{1,3},{2,0},{3,1},{4,6},{5,7},{6,4},{7,5},{8,10},{9,11},{10,... | collective-permute-start | bytes 393224 | tf_op jit(solution)/shard_map/ppermute | solution.py:233
  78.6 1.0 collective-permute-start.5
  79.6 4.7 %collective-permute-start.6 = (f32[4,64,128]{2,1,0:T(8,128)}, f32[4,64,128]{2,1,0:T(8,128)S(1)}, u32[]{:S(2)}, u32[]{:S(2)}) collective-permute-start(f32[4,64,128]{2,1,0:T(8,128)} %get-tuple-element.46), channel_id=1, source_target_pairs={{0,4},{1,5},{2,6},{3,7},{4,0},{5,1},{6,2},{7,3},{8,12},{9,13},{10,... | collective-permute-start | bytes 393224 | tf_op jit(solution)/shard_map/ppermute | solution.py:233
  84.3 0.4 collective-permute-start.7
  84.6 3.6 %collective-permute-start.8 = (f32[4,64,128]{2,1,0:T(8,128)}, f32[4,64,128]{2,1,0:T(8,128)S(1)}, u32[]{:S(2)}, u32[]{:S(2)}) collective-permute-start(f32[4,64,128]{2,1,0:T(8,128)} %get-tuple-element.48), channel_id=1, source_target_pairs={{0,6},{1,7},{2,4},{3,5},{4,2},{5,3},{6,0},{7,1},{8,14},{9,15},{10,... | collective-permute-start | bytes 393224 | tf_op jit(solution)/shard_map/ppermute | solution.py:233
  88.2 8.0 %collective-permute-done.4.refs_9_ = f32[4,64,128]{2,1,0:T(8,128)S(1)} collective-permute-done((f32[4,64,128]{2,1,0:T(8,128)}, f32[4,64,128]{2,1,0:T(8,128)S(1)}, u32[]{:S(2)}, u32[]{:S(2)}) %collective-permute-start.4) | collective-permute-done | bytes 131104 | tf_op jit(solution)/shard_map/ppermute | solution.py:233
  96.3 3.0 %collective-permute-start.9 = (f32[4,64,128]{2,1,0:T(8,128)}, f32[4,64,128]{2,1,0:T(8,128)S(1)}, u32[]{:S(2)}, u32[]{:S(2)}) collective-permute-start(f32[4,64,128]{2,1,0:T(8,128)} %get-tuple-element.49), channel_id=1, source_target_pairs={{0,7},{1,6},{2,5},{3,4},{4,3},{5,2},{6,1},{7,0},{8,15},{9,14},{10,... | collective-permute-start | bytes 393224 | tf_op jit(solution)/shard_map/ppermute | solution.py:233
  99.2 0.1 collective-permute-done.6.refs_11_
  99.4 4.3 %collective-permute-done.7.refs_12_ = f32[4,64,128]{2,1,0:T(8,128)S(1)} collective-permute-done((f32[4,64,128]{2,1,0:T(8,128)}, f32[4,64,128]{2,1,0:T(8,128)S(1)}, u32[]{:S(2)}, u32[]{:S(2)}) %collective-permute-start.7) | collective-permute-done | bytes 131104 | tf_op jit(solution)/shard_map/ppermute | solution.py:233
  103.6 3.4 %collective-permute-done.9.refs_14_ = f32[4,64,128]{2,1,0:T(8,128)S(1)} collective-permute-done((f32[4,64,128]{2,1,0:T(8,128)}, f32[4,64,128]{2,1,0:T(8,128)S(1)}, u32[]{:S(2)}, u32[]{:S(2)}) %collective-permute-start.9) | collective-permute-done | bytes 131104 | tf_op jit(solution)/shard_map/ppermute | solution.py:233
  107.0 0.6 copy-done.13
  107.6 5.5 %inv.1 = (f32[264,128]{1,0:T(8,128)}, f32[264,128]{1,0:T(8,128)}, f32[264,128]{1,0:T(8,128)}, f32[264,128]{1,0:T(8,128)}) custom-call(f32[2048,256]{1,0:T(8,128)} %get-tuple-element.38.refs_0_, f32[8,128]{1,0:T(8,128)} %get-tuple-element.37.refs_1_.dep, bf16[32,384]{1,0:T(8,128)(2,1)} %constant.17.clone.refs_2_, f32[64,256]{1,0:T(8,128)} %constant.18.clone.tc.refs_3_, ...), custom_call_target="tpu_custom_call" | custom-call | tf_op jit(solution)/shard_map/inv/pallas_call | solution.py:270
  113.2 0.0 collective-permute-start.10
  113.2 2.5 %collective-permute-start.11 = (f32[264,128]{1,0:T(8,128)}, f32[264,128]{1,0:T(8,128)S(1)}, u32[]{:S(2)}, u32[]{:S(2)}) collective-permute-start(f32[264,128]{1,0:T(8,128)} %get-tuple-element.52), channel_id=1, source_target_pairs={{0,16},{1,17},{2,18},{3,19},{4,20},{5,21},{6,22},{7,23},{8,24},{9,... | collective-permute-start | bytes 405512 | tf_op jit(solution)/shard_map/ppermute | solution.py:233
  115.7 2.2 %collective-permute-start.12 = (f32[264,128]{1,0:T(8,128)}, f32[264,128]{1,0:T(8,128)S(1)}, u32[]{:S(2)}, u32[]{:S(2)}) collective-permute-start(f32[264,128]{1,0:T(8,128)} %get-tuple-element.53), channel_id=1, source_target_pairs={{0,24},{1,25},{2,26},{3,27},{4,28},{5,29},{6,30},{7,31},{8,16},{9,... | collective-permute-start | bytes 405512 | tf_op jit(solution)/shard_map/ppermute | solution.py:233
  117.9 1.3 collective-permute-done.10.refs_1_
  119.2 2.2 %collective-permute-done.11.refs_2_ = f32[264,128]{1,0:T(8,128)S(1)} collective-permute-done((f32[264,128]{1,0:T(8,128)}, f32[264,128]{1,0:T(8,128)S(1)}, u32[]{:S(2)}, u32[]{:S(2)}) %collective-permute-start.11) | collective-permute-done | bytes 135200 | tf_op jit(solution)/shard_map/ppermute | solution.py:233
  121.4 1.7 %collective-permute-done.12.refs_3_ = f32[264,128]{1,0:T(8,128)S(1)} collective-permute-done((f32[264,128]{1,0:T(8,128)}, f32[264,128]{1,0:T(8,128)S(1)}, u32[]{:S(2)}, u32[]{:S(2)}) %collective-permute-start.12) | collective-permute-done | bytes 135200 | tf_op jit(solution)/shard_map/ppermute | solution.py:233
  123.1 0.6 copy-done.6
  123.8 1.9 %turn_out.1 = (f32[136,128]{1,0:T(8,128)}, f32[136,128]{1,0:T(8,128)}, f32[136,128]{1,0:T(8,128)}, f32[136,128]{1,0:T(8,128)}, f32[136,128]{1,0:T(8,128)}, /*ind...) custom-call(f32[8,128]{1,0:T(8,128)} %get-tuple-element.37.refs_1_.dep, ...), custom_call_target="tpu_custom_call" | custom-call | tf_op jit(solution)/shard_map/turn_out/pallas_call | solution.py:283
  125.7 0.0 collective-permute-start.13
  125.7 3.5 %collective-permute-start.14 = (f32[136,128]{1,0:T(8,128)}, f32[136,128]{1,0:T(8,128)S(1)}, u32[]{:S(2)}, u32[]{:S(2)}) collective-permute-start(f32[136,128]{1,0:T(8,128)} %get-tuple-element.56), channel_id=1, source_target_pairs={{0,2},{1,3},{2,0},{3,1},{4,6},{5,7},{6,4},{7,5},{8,10},{9,11},{10,... | collective-permute-start | bytes 208904 | tf_op jit(solution)/shard_map/ppermute | solution.py:233
  129.2 0.9 collective-permute-start.15
  130.1 3.5 %collective-permute-start.16 = (f32[136,128]{1,0:T(8,128)}, f32[136,128]{1,0:T(8,128)S(1)}, u32[]{:S(2)}, u32[]{:S(2)}) collective-permute-start(f32[136,128]{1,0:T(8,128)} %get-tuple-element.58), channel_id=1, source_target_pairs={{0,4},{1,5},{2,6},{3,7},{4,0},{5,1},{6,2},{7,3},{8,12},{9,13},{10,... | collective-permute-start | bytes 208904 | tf_op jit(solution)/shard_map/ppermute | solution.py:233
  133.6 0.6 collective-permute-start.17
  134.2 4.1 %collective-permute-start.18 = (f32[136,128]{1,0:T(8,128)}, f32[136,128]{1,0:T(8,128)S(1)}, u32[]{:S(2)}, u32[]{:S(2)}) collective-permute-start(f32[136,128]{1,0:T(8,128)} %get-tuple-element.60), channel_id=1, source_target_pairs={{0,6},{1,7},{2,4},{3,5},{4,2},{5,3},{6,0},{7,1},{8,14},{9,15},{10,... | collective-permute-start | bytes 208904 | tf_op jit(solution)/shard_map/ppermute | solution.py:233
  138.3 0.9 collective-permute-start.19
  139.3 3.2 %collective-permute-done.17.refs_5_ = f32[136,128]{1,0:T(8,128)S(1)} collective-permute-done((f32[136,128]{1,0:T(8,128)}, f32[136,128]{1,0:T(8,128)S(1)}, u32[]{:S(2)}, u32[]{:S(2)}) %collective-permute-start.17) | collective-permute-done | bytes 69664 | tf_op jit(solution)/shard_map/ppermute | solution.py:233
  142.5 1.4 collective-permute-done.18.refs_6_
  143.9 3.2 %collective-permute-done.19.refs_7_ = f32[136,128]{1,0:T(8,128)S(1)} collective-permute-done((f32[136,128]{1,0:T(8,128)}, f32[136,128]{1,0:T(8,128)S(1)}, u32[]{:S(2)}, u32[]{:S(2)}) %collective-permute-start.19) | collective-permute-done | bytes 69664 | tf_op jit(solution)/shard_map/ppermute | solution.py:233
  147.1 0.6 copy-done.20
  147.7 2.3 %post.1 = (bf16[128,512]{1,0:T(8,128)(2,1)}, bf16[128,512]{1,0:T(8,128)(2,1)}, bf16[128,512]{1,0:T(8,128)(2,1)}, f32[1,512]{1,0:T(1,128)}) custom-call(f32[136,128]{1,0:T(8,128)} %get-tuple-element.54.refs_0_, f32[136,128]{1,0:T(8,128)} %copy-done.14, f32[136,128]{1,0:T(8,128)} %copy-done.15, f32[136,128]{1,0:T(8,128)} %copy-done.16, f32[136,128]{1,0:T(8,128)} %copy-done.17, ...), custom_call_target="tpu_custom_call" | custom-call | tf_op jit(solution)/shard_map/post/pallas_call | solution.py:299
  150.0 1.0 copy-done
  151.0 3.6 %dfilt.1 = f32[2,2,1,128,512]{4,3,2,1,0:T(8,128)} custom-call(f32[32,64,128]{2,1,0:T(8,128)} %copy-done), custom_call_target="tpu_custom_call" | custom-call | tf_op jit(solution)/shard_map/dfilt/pallas_call | solution.py:290
  (51 shorter events, 0.1 us)
Async XLA Ops:
  6.2 39.4 %copy-start.23 = (f32[8,64,128]{2,1,0:T(8,128)S(1)}, f32[8,64,128]{2,1,0:T(8,128)}, u32[]{:S(2)}) copy-start(f32[8,64,128]{2,1,0:T(8,128)} %get-tuple-element.39) | copy-start | bytes 786436
  6.2 41.3 %copy-start.22 = (f32[8,64,128]{2,1,0:T(8,128)S(1)}, f32[8,64,128]{2,1,0:T(8,128)}, u32[]{:S(2)}) copy-start(f32[8,64,128]{2,1,0:T(8,128)} %get-tuple-element.40) | copy-start | bytes 786436
  6.2 44.0 %copy-start.21 = (f32[8,64,128]{2,1,0:T(8,128)S(1)}, f32[8,64,128]{2,1,0:T(8,128)}, u32[]{:S(2)}) copy-start(f32[8,64,128]{2,1,0:T(8,128)} %get-tuple-element.41) | copy-start | bytes 786436
  39.8 110.2 %all-to-all-start.1 = ((f32[32,64,128]{2,1,0:T(8,128)}), f32[32,64,128]{2,1,0:T(8,128)S(1)}, u32[]{:S(2)}, u32[]{:S(2)}) async-start(f32[32,64,128]{2,1,0:T(8,128)} %bitcast.5), calls=%async_computation.1 | async-start | bytes 2097152 | tf_op jit(solution)/shard_map/all_to_all | solution.py:228
  45.6 15.4 %collective-permute-start = (f32[8,64,128]{2,1,0:T(8,128)S(1)}, f32[8,64,128]{2,1,0:T(8,128)S(1)}, u32[]{:S(2)}, u32[]{:S(2)}) collective-permute-start(f32[8,64,128]{2,1,0:T(8,128)S(1)} %copy-done.23), channel_id=1, source_target_pairs={{0,8},{1,9},{2,10},{3,11},{4,12},{5,13},{6,14},{7,15},{8,0},{9,1},... | collective-permute-start | bytes 786440 | tf_op jit(solution)/shard_map/ppermute | solution.py:233
  47.5 22.9 %collective-permute-start.1 = (f32[8,64,128]{2,1,0:T(8,128)S(1)}, f32[8,64,128]{2,1,0:T(8,128)S(1)}, u32[]{:S(2)}, u32[]{:S(2)}) collective-permute-start(f32[8,64,128]{2,1,0:T(8,128)S(1)} %copy-done.22), channel_id=1, source_target_pairs={{0,16},{1,17},{2,18},{3,19},{4,20},{5,21},{6,22},{7,23},{8,24},{9,... | collective-permute-start | bytes 786440 | tf_op jit(solution)/shard_map/ppermute | solution.py:233
  50.2 21.9 %collective-permute-start.2 = (f32[8,64,128]{2,1,0:T(8,128)S(1)}, f32[8,64,128]{2,1,0:T(8,128)S(1)}, u32[]{:S(2)}, u32[]{:S(2)}) collective-permute-start(f32[8,64,128]{2,1,0:T(8,128)S(1)} %copy-done.21), channel_id=1, source_target_pairs={{0,24},{1,25},{2,26},{3,27},{4,28},{5,29},{6,30},{7,31},{8,16},{9,... | collective-permute-start | bytes 786440 | tf_op jit(solution)/shard_map/ppermute | solution.py:233
  61.0 11.2 %copy-start.1 = (f32[8,64,128]{2,1,0:T(8,128)}, f32[8,64,128]{2,1,0:T(8,128)S(1)}, u32[]{:S(2)}) copy-start(f32[8,64,128]{2,1,0:T(8,128)S(1)} %collective-permute-done.refs_1_) | copy-start | bytes 786436
  70.4 1.7 %copy-start.2 = (f32[8,64,128]{2,1,0:T(8,128)}, f32[8,64,128]{2,1,0:T(8,128)S(1)}, u32[]{:S(2)}) copy-start(f32[8,64,128]{2,1,0:T(8,128)S(1)} %collective-permute-done.1.refs_2_) | copy-start | bytes 786436
  72.1 0.7 copy-start.3
  75.0 9.6 %collective-permute-start.3 = (f32[4,64,128]{2,1,0:T(8,128)}, f32[4,64,128]{2,1,0:T(8,128)S(1)}, u32[]{:S(2)}, u32[]{:S(2)}) collective-permute-start(f32[4,64,128]{2,1,0:T(8,128)} %get-tuple-element.43), channel_id=1, source_target_pairs={{0,1},{1,0},{2,3},{3,2},{4,5},{5,4},{6,7},{7,6},{8,9},{9,8},{10,11... | collective-permute-start | bytes 393224 | tf_op jit(solution)/shard_map/ppermute | solution.py:233
  75.4 20.9 %collective-permute-start.4 = (f32[4,64,128]{2,1,0:T(8,128)}, f32[4,64,128]{2,1,0:T(8,128)S(1)}, u32[]{:S(2)}, u32[]{:S(2)}) collective-permute-start(f32[4,64,128]{2,1,0:T(8,128)} %get-tuple-element.44), channel_id=1, source_target_pairs={{0,2},{1,3},{2,0},{3,1},{4,6},{5,7},{6,4},{7,5},{8,10},{9,11},{10,... | collective-permute-start | bytes 393224 | tf_op jit(solution)/shard_map/ppermute | solution.py:233
  78.6 20.6 %collective-permute-start.5 = (f32[4,64,128]{2,1,0:T(8,128)}, f32[4,64,128]{2,1,0:T(8,128)S(1)}, u32[]{:S(2)}, u32[]{:S(2)}) collective-permute-start(f32[4,64,128]{2,1,0:T(8,128)} %get-tuple-element.45), channel_id=1, source_target_pairs={{0,3},{1,2},{2,1},{3,0},{4,7},{5,6},{6,5},{7,4},{8,11},{9,10},{10,... | collective-permute-start | bytes 393224 | tf_op jit(solution)/shard_map/ppermute | solution.py:233
  79.6 19.8 %collective-permute-start.6 = (f32[4,64,128]{2,1,0:T(8,128)}, f32[4,64,128]{2,1,0:T(8,128)S(1)}, u32[]{:S(2)}, u32[]{:S(2)}) collective-permute-start(f32[4,64,128]{2,1,0:T(8,128)} %get-tuple-element.46), channel_id=1, source_target_pairs={{0,4},{1,5},{2,6},{3,7},{4,0},{5,1},{6,2},{7,3},{8,12},{9,13},{10,... | collective-permute-start | bytes 393224 | tf_op jit(solution)/shard_map/ppermute | solution.py:233
  84.3 19.4 %collective-permute-start.7 = (f32[4,64,128]{2,1,0:T(8,128)}, f32[4,64,128]{2,1,0:T(8,128)S(1)}, u32[]{:S(2)}, u32[]{:S(2)}) collective-permute-start(f32[4,64,128]{2,1,0:T(8,128)} %get-tuple-element.47), channel_id=1, source_target_pairs={{0,5},{1,4},{2,7},{3,6},{4,1},{5,0},{6,3},{7,2},{8,13},{9,12},{10,... | collective-permute-start | bytes 393224 | tf_op jit(solution)/shard_map/ppermute | solution.py:233
  84.6 22.4 %copy-start.7 = (f32[4,64,128]{2,1,0:T(8,128)}, f32[4,64,128]{2,1,0:T(8,128)S(1)}, u32[]{:S(2)}) copy-start(f32[4,64,128]{2,1,0:T(8,128)S(1)} %collective-permute-done.3.refs_8_) | copy-start | bytes 393220
  84.6 19.0 %collective-permute-start.8 = (f32[4,64,128]{2,1,0:T(8,128)}, f32[4,64,128]{2,1,0:T(8,128)S(1)}, u32[]{:S(2)}, u32[]{:S(2)}) collective-permute-start(f32[4,64,128]{2,1,0:T(8,128)} %get-tuple-element.48), channel_id=1, source_target_pairs={{0,6},{1,7},{2,4},{3,5},{4,2},{5,3},{6,0},{7,1},{8,14},{9,15},{10,... | collective-permute-start | bytes 393224 | tf_op jit(solution)/shard_map/ppermute | solution.py:233
  96.3 10.7 %copy-start.8 = (f32[4,64,128]{2,1,0:T(8,128)}, f32[4,64,128]{2,1,0:T(8,128)S(1)}, u32[]{:S(2)}) copy-start(f32[4,64,128]{2,1,0:T(8,128)S(1)} %collective-permute-done.4.refs_9_) | copy-start | bytes 393220
  96.3 10.7 %collective-permute-start.9 = (f32[4,64,128]{2,1,0:T(8,128)}, f32[4,64,128]{2,1,0:T(8,128)S(1)}, u32[]{:S(2)}, u32[]{:S(2)}) collective-permute-start(f32[4,64,128]{2,1,0:T(8,128)} %get-tuple-element.49), channel_id=1, source_target_pairs={{0,7},{1,6},{2,5},{3,4},{4,3},{5,2},{6,1},{7,0},{8,15},{9,14},{10,... | collective-permute-start | bytes 393224 | tf_op jit(solution)/shard_map/ppermute | solution.py:233
  99.2 7.8 %copy-start.9 = (f32[4,64,128]{2,1,0:T(8,128)}, f32[4,64,128]{2,1,0:T(8,128)S(1)}, u32[]{:S(2)}) copy-start(f32[4,64,128]{2,1,0:T(8,128)S(1)} %collective-permute-done.5.refs_10_) | copy-start | bytes 393220
  99.4 7.6 %copy-start.10 = (f32[4,64,128]{2,1,0:T(8,128)}, f32[4,64,128]{2,1,0:T(8,128)S(1)}, u32[]{:S(2)}) copy-start(f32[4,64,128]{2,1,0:T(8,128)S(1)} %collective-permute-done.6.refs_11_) | copy-start | bytes 393220
  103.6 3.4 %copy-start.11 = (f32[4,64,128]{2,1,0:T(8,128)}, f32[4,64,128]{2,1,0:T(8,128)S(1)}, u32[]{:S(2)}) copy-start(f32[4,64,128]{2,1,0:T(8,128)S(1)} %collective-permute-done.7.refs_12_) | copy-start | bytes 393220
  103.6 3.4 %copy-start.12 = (f32[4,64,128]{2,1,0:T(8,128)}, f32[4,64,128]{2,1,0:T(8,128)S(1)}, u32[]{:S(2)}) copy-start(f32[4,64,128]{2,1,0:T(8,128)S(1)} %collective-permute-done.8.refs_13_) | copy-start | bytes 393220
  107.0 0.7 copy-start.13
  113.2 6.0 %collective-permute-start.10 = (f32[264,128]{1,0:T(8,128)}, f32[264,128]{1,0:T(8,128)S(1)}, u32[]{:S(2)}, u32[]{:S(2)}) collective-permute-start(f32[264,128]{1,0:T(8,128)} %get-tuple-element.51), channel_id=1, source_target_pairs={{0,8},{1,9},{2,10},{3,11},{4,12},{5,13},{6,14},{7,15},{8,0},{9,1},... | collective-permute-start | bytes 405512 | tf_op jit(solution)/shard_map/ppermute | solution.py:233
  113.2 8.2 %collective-permute-start.11 = (f32[264,128]{1,0:T(8,128)}, f32[264,128]{1,0:T(8,128)S(1)}, u32[]{:S(2)}, u32[]{:S(2)}) collective-permute-start(f32[264,128]{1,0:T(8,128)} %get-tuple-element.52), channel_id=1, source_target_pairs={{0,16},{1,17},{2,18},{3,19},{4,20},{5,21},{6,22},{7,23},{8,24},{9,... | collective-permute-start | bytes 405512 | tf_op jit(solution)/shard_map/ppermute | solution.py:233
  115.7 7.4 %collective-permute-start.12 = (f32[264,128]{1,0:T(8,128)}, f32[264,128]{1,0:T(8,128)S(1)}, u32[]{:S(2)}, u32[]{:S(2)}) collective-permute-start(f32[264,128]{1,0:T(8,128)} %get-tuple-element.53), channel_id=1, source_target_pairs={{0,24},{1,25},{2,26},{3,27},{4,28},{5,29},{6,30},{7,31},{8,16},{9,... | collective-permute-start | bytes 405512 | tf_op jit(solution)/shard_map/ppermute | solution.py:233
  119.2 4.0 %copy-start.4 = (f32[264,128]{1,0:T(8,128)}, f32[264,128]{1,0:T(8,128)S(1)}, u32[]{:S(2)}) copy-start(f32[264,128]{1,0:T(8,128)S(1)} %collective-permute-done.10.refs_1_) | copy-start | bytes 405508
  121.4 1.7 %copy-start.5 = (f32[264,128]{1,0:T(8,128)}, f32[264,128]{1,0:T(8,128)S(1)}, u32[]{:S(2)}) copy-start(f32[264,128]{1,0:T(8,128)S(1)} %collective-permute-done.11.refs_2_) | copy-start | bytes 405508
  123.1 0.7 copy-start.6
  125.7 8.5 %collective-permute-start.13 = (f32[136,128]{1,0:T(8,128)}, f32[136,128]{1,0:T(8,128)S(1)}, u32[]{:S(2)}, u32[]{:S(2)}) collective-permute-start(f32[136,128]{1,0:T(8,128)} %get-tuple-element.55), channel_id=1, source_target_pairs={{0,1},{1,0},{2,3},{3,2},{4,5},{5,4},{6,7},{7,6},{8,9},{9,8},{10,11... | collective-permute-start | bytes 208904 | tf_op jit(solution)/shard_map/ppermute | solution.py:233
  125.7 12.6 %collective-permute-start.14 = (f32[136,128]{1,0:T(8,128)}, f32[136,128]{1,0:T(8,128)S(1)}, u32[]{:S(2)}, u32[]{:S(2)}) collective-permute-start(f32[136,128]{1,0:T(8,128)} %get-tuple-element.56), channel_id=1, source_target_pairs={{0,2},{1,3},{2,0},{3,1},{4,6},{5,7},{6,4},{7,5},{8,10},{9,11},{10,... | collective-permute-start | bytes 208904 | tf_op jit(solution)/shard_map/ppermute | solution.py:233
  129.2 10.1 %collective-permute-start.15 = (f32[136,128]{1,0:T(8,128)}, f32[136,128]{1,0:T(8,128)S(1)}, u32[]{:S(2)}, u32[]{:S(2)}) collective-permute-start(f32[136,128]{1,0:T(8,128)} %get-tuple-element.57), channel_id=1, source_target_pairs={{0,3},{1,2},{2,1},{3,0},{4,7},{5,6},{6,5},{7,4},{8,11},{9,10},{10,... | collective-permute-start | bytes 208904 | tf_op jit(solution)/shard_map/ppermute | solution.py:233
  130.1 9.2 %collective-permute-start.16 = (f32[136,128]{1,0:T(8,128)}, f32[136,128]{1,0:T(8,128)S(1)}, u32[]{:S(2)}, u32[]{:S(2)}) collective-permute-start(f32[136,128]{1,0:T(8,128)} %get-tuple-element.58), channel_id=1, source_target_pairs={{0,4},{1,5},{2,6},{3,7},{4,0},{5,1},{6,2},{7,3},{8,12},{9,13},{10,... | collective-permute-start | bytes 208904 | tf_op jit(solution)/shard_map/ppermute | solution.py:233
  133.6 8.9 %collective-permute-start.17 = (f32[136,128]{1,0:T(8,128)}, f32[136,128]{1,0:T(8,128)S(1)}, u32[]{:S(2)}, u32[]{:S(2)}) collective-permute-start(f32[136,128]{1,0:T(8,128)} %get-tuple-element.59), channel_id=1, source_target_pairs={{0,5},{1,4},{2,7},{3,6},{4,1},{5,0},{6,3},{7,2},{8,13},{9,12},{10,... | collective-permute-start | bytes 208904 | tf_op jit(solution)/shard_map/ppermute | solution.py:233
  134.2 12.9 %copy-start.14 = (f32[136,128]{1,0:T(8,128)}, f32[136,128]{1,0:T(8,128)S(1)}, u32[]{:S(2)}) copy-start(f32[136,128]{1,0:T(8,128)S(1)} %collective-permute-done.13.refs_1_) | copy-start | bytes 208900
  134.2 9.6 %collective-permute-start.18 = (f32[136,128]{1,0:T(8,128)}, f32[136,128]{1,0:T(8,128)S(1)}, u32[]{:S(2)}, u32[]{:S(2)}) collective-permute-start(f32[136,128]{1,0:T(8,128)} %get-tuple-element.60), channel_id=1, source_target_pairs={{0,6},{1,7},{2,4},{3,5},{4,2},{5,3},{6,0},{7,1},{8,14},{9,15},{10,... | collective-permute-start | bytes 208904 | tf_op jit(solution)/shard_map/ppermute | solution.py:233
  138.3 8.8 %copy-start.15 = (f32[136,128]{1,0:T(8,128)}, f32[136,128]{1,0:T(8,128)S(1)}, u32[]{:S(2)}) copy-start(f32[136,128]{1,0:T(8,128)S(1)} %collective-permute-done.14.refs_2_) | copy-start | bytes 208900
  138.3 8.8 %collective-permute-start.19 = (f32[136,128]{1,0:T(8,128)}, f32[136,128]{1,0:T(8,128)S(1)}, u32[]{:S(2)}, u32[]{:S(2)}) collective-permute-start(f32[136,128]{1,0:T(8,128)} %get-tuple-element.61), channel_id=1, source_target_pairs={{0,7},{1,6},{2,5},{3,4},{4,3},{5,2},{6,1},{7,0},{8,15},{9,14},{10,... | collective-permute-start | bytes 208904 | tf_op jit(solution)/shard_map/ppermute | solution.py:233
  139.3 7.8 %copy-start.16 = (f32[136,128]{1,0:T(8,128)}, f32[136,128]{1,0:T(8,128)S(1)}, u32[]{:S(2)}) copy-start(f32[136,128]{1,0:T(8,128)S(1)} %collective-permute-done.15.refs_3_) | copy-start | bytes 208900
  139.3 7.8 %copy-start.17 = (f32[136,128]{1,0:T(8,128)}, f32[136,128]{1,0:T(8,128)S(1)}, u32[]{:S(2)}) copy-start(f32[136,128]{1,0:T(8,128)S(1)} %collective-permute-done.16.refs_4_) | copy-start | bytes 208900
  142.5 4.6 %copy-start.18 = (f32[136,128]{1,0:T(8,128)}, f32[136,128]{1,0:T(8,128)S(1)}, u32[]{:S(2)}) copy-start(f32[136,128]{1,0:T(8,128)S(1)} %collective-permute-done.17.refs_5_) | copy-start | bytes 208900
  143.8 3.3 %copy-start.19 = (f32[136,128]{1,0:T(8,128)}, f32[136,128]{1,0:T(8,128)S(1)}, u32[]{:S(2)}) copy-start(f32[136,128]{1,0:T(8,128)S(1)} %collective-permute-done.18.refs_6_) | copy-start | bytes 208900
  147.1 0.6 copy-start.20
  150.0 1.0 copy-start
